TPU v7x, 1024 devices: a whole 4x4x32 slice. The times are simulated.
1024 devices in a mesh: gz: 16 (over z_lo), gy: 8 (over y, z_hi), gx: 8 (over x, core).
Axes of the slice: x: 4, y: 4, z: 32 (z_hi: 2, z_lo: 16; z = z_hi * 16 + z_lo), core: 2. Of those that a mesh axis runs over, the one named last changes fastest.
Arguments:
- positions: float32 [3, 48, 24, 24, 128], P(None, 'gz', 'gy', 'gx'), may hold values from 0 to 1
- velocities: float32 [3, 48, 24, 24, 128], P(None, 'gz', 'gy', 'gx'), may hold values from -6 to 6
- counts: int32 [48, 24, 24], P('gz', 'gy', 'gx'), may hold values from 64 to 128
- bonds: int32 [2, 48, 24, 24, 128], P(None, 'gz', 'gy', 'gx'), may hold values from 0 to 127
- plan_z: int32 [16], replicated, may hold values from 0 to 2
- plan_y: int32 [16, 8], replicated, may hold values from 0 to 2
- plan_x: int32 [16, 8, 8], replicated, may hold values from 0 to 2
Outputs:
- forces_first: float32 [3, 48, 24, 24, 128], P(None, 'gz', 'gy', 'gx')
- moved_positions: float32 [3, 80, 40, 40, 128], P(None, 'gz', 'gy', 'gx')
- moved_forces: float32 [3, 80, 40, 40, 128], P(None, 'gz', 'gy', 'gx')
Inputs may be any that keep to these rules, and one draw needn't show every extreme that they name: `counts`: bead b of a cell is present when b is less than the cell's count. `bonds`: both ends of a bond are bead places of the bond's own cell; a bond counts only when both ends are present. `plan_z`: entry i is the number of cells by which the boundary between brick planes i and i + 1 (the last with plane 0) moves up. `plan_y`: entry (i, j) is the number of cells by which the boundary between columns j and j + 1 of plane i (the last with column 0) moves up. `plan_x`: entry (i, j, k) is the number of cells by which the boundary between bricks k and k + 1 of column (i, j) (the last with brick 0) moves up.
All inputs are finite; a program needn't handle non-finite values.
Results may differ from a plain program's by a relative error of at most 0.0001.
Values sent between devices are 32-bit elements; how exact they have to be, the bound alone decides.
No kernel may reach another device: no remote copies, remote signals or barrier semaphores. Data moves between devices by JAX's collectives and lax.ppermute only.
A program may use at most 32 MiB of HBM per device.

v0:
```python
import jax
import jax.numpy as jnp
from jax import lax
from jax.sharding import PartitionSpec as P

STRENGTH = 0.3
SPREAD = 0.6
BOND_STIFF = 1.0
STEP_DT = 0.2
FAR_AWAY = 1000.0
ALL_OFFSETS = [
    (along_z, along_y, along_x)
    for along_z in (-1, 0, 1)
    for along_y in (-1, 0, 1)
    for along_x in (-1, 0, 1)
]
HALF_OFFSETS = [offset for offset in ALL_OFFSETS if offset > (0, 0, 0)]


def from_behind(block, axis, distance):
    devices = range(lax.axis_size(axis))
    route = [((i - distance) % len(devices), i) for i in devices]
    return lax.ppermute(block, axis, route)


def pair_term(own_beads, partner, offset):
    offset_vec = jnp.array(offset, dtype=jnp.float32).reshape(3, 1, 1, 1)
    separation = own_beads[:, :, :, None] - partner[:, :, None, :] - offset_vec
    distance = jnp.sum(separation * separation, axis=0)
    return (STRENGTH * jnp.exp(-distance / SPREAD))[None] * separation


def pair_sums(first_cube, second_cube, offset):
    planes_first = jnp.moveaxis(first_cube, 1, 0)
    planes_second = jnp.moveaxis(second_cube, 1, 0)

    def pair_one_plane(pieces):
        side_a = pieces[0].reshape(3, -1, pieces[0].shape[-1])
        side_b = pieces[1].reshape(3, -1, pieces[1].shape[-1])
        pushes = pair_term(side_a, side_b, offset)
        return (
            jnp.sum(pushes, axis=3).reshape(pieces[0].shape),
            jnp.sum(pushes, axis=2).reshape(pieces[0].shape),
        )

    on_first, on_second = lax.map(pair_one_plane, (planes_first, planes_second))
    return (jnp.moveaxis(on_first, 0, 1), jnp.moveaxis(on_second, 0, 1))


def bond_plane(coords, living, bonds):
    bead_count = coords.shape[-1]
    bond_count = bonds.shape[-1]
    bead_index = jnp.arange(bead_count, dtype=jnp.int32)
    head_pick = (bonds[0].reshape(-1, bond_count)[:, :, None] == bead_index).astype(jnp.float32)
    tail_pick = (bonds[1].reshape(-1, bond_count)[:, :, None] == bead_index).astype(jnp.float32)
    flat_coords = coords.reshape(3, -1, bead_count)
    flat_alive = living.reshape(-1, bead_count)
    head_pos = jnp.einsum("kcb,cnb->kcn", flat_coords, head_pick, precision=lax.Precision.HIGHEST)
    tail_pos = jnp.einsum("kcb,cnb->kcn", flat_coords, tail_pick, precision=lax.Precision.HIGHEST)
    head_alive = jnp.einsum("cb,cnb->cn", flat_alive, head_pick, precision=lax.Precision.HIGHEST)
    tail_alive = jnp.einsum("cb,cnb->cn", flat_alive, tail_pick, precision=lax.Precision.HIGHEST)
    tension = BOND_STIFF * (head_alive * tail_alive)[None] * (tail_pos - head_pos)
    return jnp.einsum(
        "kcn,cnb->kcb", tension, head_pick - tail_pick, precision=lax.Precision.HIGHEST
    ).reshape(coords.shape)


def bond_term(coords, living, bonds):

    def bond_one_plane(pieces):
        return bond_plane(pieces[0], pieces[1], pieces[2])

    planes = lax.map(
        bond_one_plane, (jnp.moveaxis(coords, 1, 0), living, jnp.moveaxis(bonds, 1, 0))
    )
    return jnp.moveaxis(planes, 0, 1)


def cube_at(blocks, start, side_cells):
    return blocks[
        :,
        start[0] : start[0] + side_cells,
        start[1] : start[1] + side_cells,
        start[2] : start[2] + side_cells,
    ]


def add_cube(backlog, start, side_cells, values):
    return backlog.at[
        :,
        start[0] : start[0] + side_cells,
        start[1] : start[1] + side_cells,
        start[2] : start[2] + side_cells,
    ].add(values)


def upper_extend(parked):
    lowest = lax.slice_in_dim(parked, 0, 1, axis=1)
    grown = jnp.concatenate([parked, from_behind(lowest, "gz", -1)], axis=1)
    lowest = lax.slice_in_dim(grown, 0, 1, axis=2)
    grown = jnp.concatenate([grown, from_behind(lowest, "gy", -1)], axis=2)
    lowest = lax.slice_in_dim(grown, 0, 1, axis=3)
    return jnp.concatenate([grown, from_behind(lowest, "gx", -1)], axis=3)


def fold_back(backlog, which_axis, side_cells, arrival):
    kept = lax.slice_in_dim(backlog, 0, side_cells, axis=which_axis)
    first_layer = lax.slice_in_dim(kept, 0, 1, axis=which_axis) + arrival
    rest = lax.slice_in_dim(kept, 1, side_cells, axis=which_axis)
    return jnp.concatenate([first_layer, rest], axis=which_axis)


def local_forces(coords, living, bonds):
    side_cells = coords.shape[1]
    parked = jnp.where(living[None] > 0, coords, FAR_AWAY)
    extended = upper_extend(parked)
    self_part, self_other = pair_sums(parked, parked, (0, 0, 0))
    backlog = jnp.zeros_like(extended)
    backlog = add_cube(backlog, (0, 0, 0), side_cells, self_part)
    for offset in HALF_OFFSETS:
        first_start = tuple((1 if part < 0 else 0 for part in offset))
        second_start = tuple((first_start[k] + offset[k] for k in range(3)))
        first_beads = cube_at(extended, first_start, side_cells)
        second_beads = cube_at(extended, second_start, side_cells)
        on_first, on_second = pair_sums(first_beads, second_beads, offset)
        backlog = add_cube(backlog, first_start, side_cells, on_first)
        backlog = add_cube(backlog, second_start, side_cells, -on_second)
    top_layer = lax.slice_in_dim(backlog, side_cells, side_cells + 1, axis=3)
    backlog = fold_back(backlog, 3, side_cells, from_behind(top_layer, "gx", 1))
    top_layer = lax.slice_in_dim(backlog, side_cells, side_cells + 1, axis=2)
    backlog = fold_back(backlog, 2, side_cells, from_behind(top_layer, "gy", 1))
    top_layer = lax.slice_in_dim(backlog, side_cells, side_cells + 1, axis=1)
    backlog = fold_back(backlog, 1, side_cells, from_behind(top_layer, "gz", 1))
    summed = backlog
    summed = summed + bond_term(coords, living, bonds)
    return summed * living[None]


def pick_entry(plan_table, position):
    matched = jnp.arange(plan_table.shape[0], dtype=jnp.int32) == position
    return jnp.sum(
        jnp.where(matched.reshape((-1,) + (1,) * (plan_table.ndim - 1)), plan_table, 0), axis=0
    )


def hand_over(blocks, arrival, which_axis, lowered, raised, side_cells):
    joined = jnp.concatenate([blocks, arrival, jnp.zeros_like(arrival)], axis=which_axis)
    kept_part = lax.dynamic_slice_in_dim(joined, lowered, side_cells + 2, axis=which_axis)
    filled = side_cells + raised - lowered
    usable = (jnp.arange(side_cells + 2, dtype=jnp.int32) < filled).astype(jnp.float32)
    shape_list = [1] * blocks.ndim
    shape_list[which_axis] = side_cells + 2
    return kept_part * usable.reshape(shape_list)


def on_device(positions, velocities, counts, bonds, plan_z, plan_y, plan_x):
    side_cells = positions.shape[1]
    bead_count = positions.shape[-1]
    living = (jnp.arange(bead_count, dtype=jnp.int32) < counts[..., None]).astype(jnp.float32)
    forces_first = local_forces(positions, living, bonds)
    stepped = positions + STEP_DT * velocities + 0.5 * STEP_DT * STEP_DT * forces_first
    forces_next = local_forces(stepped, living, bonds)
    carried = jnp.concatenate([stepped * living[None], forces_next], axis=0)
    plane_index = lax.axis_index("gz")
    column_index = lax.axis_index("gy")
    brick_index = lax.axis_index("gx")
    plane_total = lax.axis_size("gz")
    column_total = lax.axis_size("gy")
    brick_total = lax.axis_size("gx")
    lowered_z = pick_entry(plan_z, (plane_index + plane_total - 1) % plane_total)
    raised_z = pick_entry(plan_z, plane_index)
    plane_row = pick_entry(plan_y, plane_index)
    lowered_y = pick_entry(plane_row, (column_index + column_total - 1) % column_total)
    raised_y = pick_entry(plane_row, column_index)
    column_row = pick_entry(pick_entry(plan_x, plane_index), column_index)
    lowered_x = pick_entry(column_row, (brick_index + brick_total - 1) % brick_total)
    raised_x = pick_entry(column_row, brick_index)
    arrival = from_behind(lax.slice_in_dim(carried, 0, 2, axis=1), "gz", -1)
    carried = hand_over(carried, arrival, 1, lowered_z, raised_z, side_cells)
    arrival = from_behind(lax.slice_in_dim(carried, 0, 2, axis=2), "gy", -1)
    carried = hand_over(carried, arrival, 2, lowered_y, raised_y, side_cells)
    arrival = from_behind(lax.slice_in_dim(carried, 0, 2, axis=3), "gx", -1)
    carried = hand_over(carried, arrival, 3, lowered_x, raised_x, side_cells)
    return (forces_first, carried[:3], carried[3:])


def solution(mesh):
    return jax.shard_map(
        on_device,
        mesh=mesh,
        in_specs=(
            P(None, "gz", "gy", "gx", None),
            P(None, "gz", "gy", "gx", None),
            P("gz", "gy", "gx"),
            P(None, "gz", "gy", "gx", None),
            P(),
            P(),
            P(),
        ),
        out_specs=(
            P(None, "gz", "gy", "gx", None),
            P(None, "gz", "gy", "gx", None),
            P(None, "gz", "gy", "gx", None),
        ),
        check_vma=False,
    )
```

profile of v0, /device:TPU:7, one launch (start us, length us, event | category | flops | bytes accessed | tf_op | source)
XLA Modules:
  0.0 397.5 jit_solution(4110865349183396452)
XLA Ops:
  2.3 26.1 %collective-permute-start = (f32[3,1,3,3,128]{4,0,3,2,1:T(4,128)S(1)}, f32[3,1,3,3,128]{4,0,3,2,1:T(4,128)S(1)}, u32[]{:S(2)}, u32[]{:S(2)}) collective-permute-start(f32[3,1,3,3,128]{4,0,3,2,1:T(4,128)S(1)} %slice.2454), channel_id=1, source_target_pairs={{64,0},{128,64},{192,128},{256,192},{320,256},{384,320},{448,384},... | collective-permute-start | bytes 41480 | tf_op jit(solution)/shard_map/ppermute | solution.py:23
  29.2 10.9 %while.436 = (s32[]{:T(128)}, f32[3,3,3,3,128]{4,1,3,2,0:T(4,128)S(1)}, s32[3,2,3,3,128]{4,3,2,1,0:T(4,128)S(1)}, f32[3,3,3,128]{3,2,1,0:T(4,128)S(1)}, f32[3,3,...) while((s32[]{:T(128)}, f32[3,3,3,3,128]{4,1,3,2,0:T(4,128)S(1)}, ...), condition=%wide.region_70.71_spmd, body=%wide.region_69.70_spmd.sunk | while | flops 20799364 | bytes 281213 | solution.py:73
  40.1 5.3 %while.438 = (s32[]{:T(128)}, f32[3,3,3,3,128]{4,1,3,2,0:T(4,128)S(1)}, f32[3,3,3,3,128]{4,1,3,2,0:T(4,128)S(1)}, s32[]{:T(128)}) while((s32[]{:T(128)}, f32[3,3,3,3,128]{4,1,3,2,0:T(4,128)S(1)}, f32[3,3,3,3,128]{4,1,3,2,0:T(4,128)S(1)}, s32[]{:T(128)}) %tuple.1039), condition=%wide.region_3.4_spmd.clone, body=%wide.region_0.3_spmd.sunk.clone.sunk | while | flops 2945666 | bytes 2520645 | solution.py:46
  45.8 14.2 %collective-permute-start.1 = (f32[3,4,1,3,128]{4,0,3,2,1:T(4,128)S(1)}, f32[3,4,1,3,128]{4,0,3,2,1:T(4,128)S(1)}, u32[]{:S(2)}, u32[]{:S(2)}) collective-permute-start(f32[3,4,1,3,128]{4,0,3,2,1:T(4,128)S(1)} %pad_maximum_fusion.10), channel_id=1, source_target_pairs={{8,0},{16,8},{24,16},{32,24},{40,32},{48,40},{56,48},{0,56},{9,1},... | collective-permute-start | bytes 55304 | tf_op jit(solution)/shard_map/ppermute | solution.py:23
  60.1 5.6 %while.447 = (s32[]{:T(128)}, f32[3,3,3,3,128]{4,1,3,2,0:T(4,128)S(1)}, f32[3,3,3,3,128]{4,1,3,2,0:T(4,128)S(1)}, f32[3,3,3,3,128]{4,1,3,2,0:T(4,128)S(1)}, f32[...) while((s32[]{:T(128)}, f32[3,3,3,3,128]{4,1,3,2,0:T(4,128)S(1)}, ...), condition=%wide.region_48.49_spmd.clone, body=%wide.region_44.0_spmd.sunk.clone.sunk | while | flops 4269314 | bytes 2681977 | solution.py:46
  65.7 3.2 collective-permute-done.1
  69.0 1.9 collective-permute-start.2
  71.0 5.6 %while.441 = (s32[]{:T(128)}, f32[3,3,3,3,128]{4,1,3,2,0:T(4,128)S(1)}, f32[3,3,3,3,128]{4,1,3,2,0:T(4,128)S(1)}, f32[3,3,3,3,128]{4,1,3,2,0:T(4,128)S(1)}, f32[...) while((s32[]{:T(128)}, f32[3,3,3,3,128]{4,1,3,2,0:T(4,128)S(1)}, ...), condition=%wide.region_18.19_spmd.clone, body=%wide.region_14.18_spmd.sunk.clone.sunk | while | flops 4269314 | bytes 2681977 | solution.py:46
  76.6 5.6 %while.444 = (s32[]{:T(128)}, f32[3,3,3,3,128]{4,1,3,2,0:T(4,128)S(1)}, f32[3,3,3,3,128]{4,1,3,2,0:T(4,128)S(1)}, f32[3,3,3,3,128]{4,1,3,2,0:T(4,128)S(1)}, f32[...) while((s32[]{:T(128)}, f32[3,3,3,3,128]{4,1,3,2,0:T(4,128)S(1)}, ...), condition=%wide.region_33.34_spmd.clone, body=%wide.region_29.33_spmd.sunk.clone.sunk | while | flops 4269314 | bytes 2681977 | solution.py:46
  82.2 5.6 %while.450 = (s32[]{:T(128)}, f32[3,3,3,3,128]{4,1,3,2,0:T(4,128)S(1)}, f32[3,3,3,3,128]{4,1,3,2,0:T(4,128)S(1)}, f32[3,3,3,3,128]{4,1,3,2,0:T(4,128)S(1)}, f32[...) while((s32[]{:T(128)}, f32[3,3,3,3,128]{4,1,3,2,0:T(4,128)S(1)}, ...), condition=%wide.region_63.64_spmd.clone, body=%wide.region_59.0_spmd.sunk.clone.sunk | while | flops 4269314 | bytes 2681977 | solution.py:46
  88.5 5.5 %while.439 = (s32[]{:T(128)}, f32[3,3,3,3,128]{4,1,3,2,0:T(4,128)S(1)}, f32[3,3,3,3,128]{4,1,3,2,0:T(4,128)S(1)}, f32[3,3,3,3,128]{4,1,3,2,0:T(4,128)S(1)}, f32[...) while((s32[]{:T(128)}, f32[3,3,3,3,128]{4,1,3,2,0:T(4,128)S(1)}, ...), condition=%wide.region_8.9_spmd.clone, body=%wide.region_4.0_spmd.sunk.clone.sunk | while | flops 4269314 | bytes 2681977 | solution.py:46
  94.1 5.6 %while.440 = (s32[]{:T(128)}, f32[3,3,3,3,128]{4,1,3,2,0:T(4,128)S(1)}, f32[3,3,3,3,128]{4,1,3,2,0:T(4,128)S(1)}, f32[3,3,3,3,128]{4,1,3,2,0:T(4,128)S(1)}, f32[...) while((s32[]{:T(128)}, f32[3,3,3,3,128]{4,1,3,2,0:T(4,128)S(1)}, ...), condition=%wide.region_13.14_spmd.clone, body=%wide.region_9.0_spmd.sunk.clone.sunk | while | flops 4269314 | bytes 2681977 | solution.py:46
  99.8 6.0 %while.442 = (s32[]{:T(128)}, f32[3,3,3,3,128]{4,1,3,2,0:T(4,128)S(1)}, f32[3,3,3,3,128]{4,1,3,2,0:T(4,128)S(1)}, f32[3,3,3,3,128]{4,1,3,2,0:T(4,128)S(1)}, f32[...) while((s32[]{:T(128)}, f32[3,3,3,3,128]{4,1,3,2,0:T(4,128)S(1)}, ...), condition=%wide.region_23.24_spmd.clone, body=%wide.region_19.23_spmd.sunk.clone.sunk | while | flops 4269314 | bytes 2681977 | solution.py:46
  106.5 5.5 %while.443 = (s32[]{:T(128)}, f32[3,3,3,3,128]{4,1,3,2,0:T(4,128)S(1)}, f32[3,3,3,3,128]{4,1,3,2,0:T(4,128)S(1)}, f32[3,3,3,3,128]{4,1,3,2,0:T(4,128)S(1)}, f32[...) while((s32[]{:T(128)}, f32[3,3,3,3,128]{4,1,3,2,0:T(4,128)S(1)}, ...), condition=%wide.region_28.29_spmd.clone, body=%wide.region_24.0_spmd.sunk.clone.sunk | while | flops 4269314 | bytes 2681977 | solution.py:46
  107.2 1.1 fusion.276
  109.1 1.1 fusion.276
  110.9 1.1 fusion.276
  112.1 5.6 %while.445 = (s32[]{:T(128)}, f32[3,3,3,3,128]{4,1,3,2,0:T(4,128)S(1)}, f32[3,3,3,3,128]{4,1,3,2,0:T(4,128)S(1)}, f32[3,3,3,3,128]{4,1,3,2,0:T(4,128)S(1)}, f32[...) while((s32[]{:T(128)}, f32[3,3,3,3,128]{4,1,3,2,0:T(4,128)S(1)}, ...), condition=%wide.region_38.39_spmd.clone, body=%wide.region_34.38_spmd.sunk.clone.sunk | while | flops 4269314 | bytes 2681977 | solution.py:46
  112.8 1.1 fusion.278
  114.7 1.1 fusion.278
  116.6 1.1 fusion.278
  117.8 5.6 %while.446 = (s32[]{:T(128)}, f32[3,3,3,3,128]{4,1,3,2,0:T(4,128)S(1)}, f32[3,3,3,3,128]{4,1,3,2,0:T(4,128)S(1)}, f32[3,3,3,3,128]{4,1,3,2,0:T(4,128)S(1)}, f32[...) while((s32[]{:T(128)}, f32[3,3,3,3,128]{4,1,3,2,0:T(4,128)S(1)}, ...), condition=%wide.region_43.44_spmd.clone, body=%wide.region_39.0_spmd.sunk.clone.sunk | while | flops 4269314 | bytes 2681977 | solution.py:46
  123.4 5.6 %while.448 = (s32[]{:T(128)}, f32[3,3,3,3,128]{4,1,3,2,0:T(4,128)S(1)}, f32[3,3,3,3,128]{4,1,3,2,0:T(4,128)S(1)}, f32[3,3,3,3,128]{4,1,3,2,0:T(4,128)S(1)}, f32[...) while((s32[]{:T(128)}, f32[3,3,3,3,128]{4,1,3,2,0:T(4,128)S(1)}, ...), condition=%wide.region_53.54_spmd.clone, body=%wide.region_49.53_spmd.sunk.clone.sunk | while | flops 4269314 | bytes 2681977 | solution.py:46
  129.0 5.6 %while.449 = (s32[]{:T(128)}, f32[3,3,3,3,128]{4,1,3,2,0:T(4,128)S(1)}, f32[3,3,3,3,128]{4,1,3,2,0:T(4,128)S(1)}, f32[3,3,3,3,128]{4,1,3,2,0:T(4,128)S(1)}, f32[...) while((s32[]{:T(128)}, f32[3,3,3,3,128]{4,1,3,2,0:T(4,128)S(1)}, ...), condition=%wide.region_58.59_spmd.clone, body=%wide.region_54.58_spmd.sunk.clone.sunk | while | flops 4269314 | bytes 2681977 | solution.py:46
  134.6 5.8 %while.451 = (s32[]{:T(128)}, f32[3,3,3,3,128]{4,1,3,2,0:T(4,128)S(1)}, f32[3,3,3,3,128]{4,1,3,2,0:T(4,128)S(1)}, f32[3,3,3,3,128]{4,1,3,2,0:T(4,128)S(1)}, f32[3,3,3,3,128]{4,1,3,2,0:T(4,128)S(1)}, /*index=5*/s32[]{:T(128)}) while((s32[]{:T(128)}, f32[3,3,3,3,128]{4,1,3,2,0:T(4,128)S(1)}, ...), condition=%wide.region_68.69_spmd.clone, body=%wide.region_64.68_spmd.sunk.clone.sunk | while | flops 4269314 | bytes 2681945 | solution.py:46
  135.5 1.1 fusion.284
  137.4 1.1 fusion.284
  139.3 1.1 fusion.284
  143.3 12.2 %collective-permute-start.4 = (f32[3,4,1,3,128]{4,0,3,2,1:T(4,128)S(1)}, f32[3,4,1,3,128]{4,0,3,2,1:T(4,128)S(1)}, u32[]{:S(2)}, u32[]{:S(2)}) collective-permute-start(f32[3,4,1,3,128]{4,0,3,2,1:T(4,128)S(1)} %pad_maximum_fusion.9), channel_id=1, source_target_pairs={{56,0},{0,8},{8,16},{16,24},{24,32},{32,40},{40,48},{48,56},{57,1}... | collective-permute-start | bytes 55304 | tf_op jit(solution)/shard_map/ppermute | solution.py:23
  155.7 12.7 %collective-permute-done.4 = f32[3,4,1,3,128]{4,0,3,2,1:T(4,128)S(1)} collective-permute-done((f32[3,4,1,3,128]{4,0,3,2,1:T(4,128)S(1)}, f32[3,4,1,3,128]{4,0,3,2,1:T(4,128)S(1)}, u32[]{:S(2)}, u32[]{:S(2)}) %collective-permute-start.4) | collective-permute-done | bytes 18464 | tf_op jit(solution)/shard_map/ppermute | solution.py:23
  168.5 1.9 collective-permute-start.5
  171.2 18.0 %collective-permute-done.5 = f32[3,1,3,3,128]{4,0,3,2,1:T(4,128)S(1)} collective-permute-done((f32[3,1,3,3,128]{4,0,3,2,1:T(4,128)S(1)}, f32[3,1,3,3,128]{4,0,3,2,1:T(4,128)S(1)}, u32[]{:S(2)}, u32[]{:S(2)}) %collective-permute-start.5) | collective-permute-done | bytes 13856 | tf_op jit(solution)/shard_map/ppermute | solution.py:23
  189.3 1.9 collective-permute-start.6
  191.3 5.3 %while.452 = (s32[]{:T(128)}, f32[3,3,3,3,128]{4,1,3,2,0:T(4,128)S(1)}, f32[3,3,3,3,128]{4,1,3,2,0:T(4,128)S(1)}, s32[]{:T(128)}) while((s32[]{:T(128)}, f32[3,3,3,3,128]{4,1,3,2,0:T(4,128)S(1)}, f32[3,3,3,3,128]{4,1,3,2,0:T(4,128)S(1)}, s32[]{:T(128)}) %tuple.1047), condition=%wide.region_74.75_spmd.clone, body=%wide.region_71.0_spmd.sunk.clone.sunk | while | flops 2945666 | bytes 2520645 | solution.py:46
  196.7 13.8 %collective-permute-start.7 = (f32[3,4,1,3,128]{4,0,3,2,1:T(4,128)S(1)}, f32[3,4,1,3,128]{4,0,3,2,1:T(4,128)S(1)}, u32[]{:S(2)}, u32[]{:S(2)}) collective-permute-start(f32[3,4,1,3,128]{4,0,3,2,1:T(4,128)S(1)} %pad_maximum_fusion.8), channel_id=1, source_target_pairs={{8,0},{16,8},{24,16},{32,24},{40,32},{48,40},{56,48},{0,56},{9,1},... | collective-permute-start | bytes 55304 | tf_op jit(solution)/shard_map/ppermute | solution.py:23
  210.5 5.6 %while.461 = (s32[]{:T(128)}, f32[3,3,3,3,128]{4,1,3,2,0:T(4,128)S(1)}, f32[3,3,3,3,128]{4,1,3,2,0:T(4,128)S(1)}, f32[3,3,3,3,128]{4,1,3,2,0:T(4,128)S(1)}, f32[...) while((s32[]{:T(128)}, f32[3,3,3,3,128]{4,1,3,2,0:T(4,128)S(1)}, ...), condition=%wide.region_119.120_spmd.clone, body=%wide.region_115.119_spmd.sunk.clone.sunk | while | flops 4269314 | bytes 2681977 | solution.py:46
  216.1 3.5 collective-permute-done.7
  219.6 5.0 %collective-permute-start.8 = (f32[3,4,4,1,128]{4,0,3,2,1:T(4,128)S(1)}, f32[3,4,4,1,128]{4,0,3,2,1:T(4,128)S(1)}, u32[]{:S(2)}, u32[]{:S(2)}) collective-permute-start(f32[3,4,4,1,128]{4,0,3,2,1:T(4,128)S(1)} %slice.2492), channel_id=1, source_target_pairs={{1,0},{2,1},{3,2},{4,3},{5,4},{6,5},{7,6},{0,7},{9,8},{10,9},{11,1... | collective-permute-start | bytes 73736 | tf_op jit(solution)/shard_map/ppermute | solution.py:23
  224.6 5.6 %while.455 = (s32[]{:T(128)}, f32[3,3,3,3,128]{4,1,3,2,0:T(4,128)S(1)}, f32[3,3,3,3,128]{4,1,3,2,0:T(4,128)S(1)}, f32[3,3,3,3,128]{4,1,3,2,0:T(4,128)S(1)}, f32[...) while((s32[]{:T(128)}, f32[3,3,3,3,128]{4,1,3,2,0:T(4,128)S(1)}, ...), condition=%wide.region_89.90_spmd.clone, body=%wide.region_85.89_spmd.sunk.clone.sunk | while | flops 4269314 | bytes 2681977 | solution.py:46
  230.2 5.6 %while.458 = (s32[]{:T(128)}, f32[3,3,3,3,128]{4,1,3,2,0:T(4,128)S(1)}, f32[3,3,3,3,128]{4,1,3,2,0:T(4,128)S(1)}, f32[3,3,3,3,128]{4,1,3,2,0:T(4,128)S(1)}, f32[...) while((s32[]{:T(128)}, f32[3,3,3,3,128]{4,1,3,2,0:T(4,128)S(1)}, ...), condition=%wide.region_104.105_spmd.clone, body=%wide.region_100.104_spmd.sunk.clone.sunk | while | flops 4269314 | bytes 2681977 | solution.py:46
  235.9 5.6 %while.464 = (s32[]{:T(128)}, f32[3,3,3,3,128]{4,1,3,2,0:T(4,128)S(1)}, f32[3,3,3,3,128]{4,1,3,2,0:T(4,128)S(1)}, f32[3,3,3,3,128]{4,1,3,2,0:T(4,128)S(1)}, f32[...) while((s32[]{:T(128)}, f32[3,3,3,3,128]{4,1,3,2,0:T(4,128)S(1)}, ...), condition=%wide.region_134.135_spmd.clone, body=%wide.region_130.134_spmd.sunk.clone.sunk | while | flops 4269314 | bytes 2681977 | solution.py:46
  241.6 5.6 %while.453 = (s32[]{:T(128)}, f32[3,3,3,3,128]{4,1,3,2,0:T(4,128)S(1)}, f32[3,3,3,3,128]{4,1,3,2,0:T(4,128)S(1)}, f32[3,3,3,3,128]{4,1,3,2,0:T(4,128)S(1)}, f32[...) while((s32[]{:T(128)}, f32[3,3,3,3,128]{4,1,3,2,0:T(4,128)S(1)}, ...), condition=%wide.region_79.80_spmd.clone, body=%wide.region_75.79_spmd.sunk.clone.sunk | while | flops 4269314 | bytes 2681977 | solution.py:46
  247.2 5.6 %while.454 = (s32[]{:T(128)}, f32[3,3,3,3,128]{4,1,3,2,0:T(4,128)S(1)}, f32[3,3,3,3,128]{4,1,3,2,0:T(4,128)S(1)}, f32[3,3,3,3,128]{4,1,3,2,0:T(4,128)S(1)}, f32[...) while((s32[]{:T(128)}, f32[3,3,3,3,128]{4,1,3,2,0:T(4,128)S(1)}, ...), condition=%wide.region_84.85_spmd.clone, body=%wide.region_80.0_spmd.sunk.clone.sunk | while | flops 4269314 | bytes 2681977 | solution.py:46
  252.8 5.8 %while.456 = (s32[]{:T(128)}, f32[3,3,3,3,128]{4,1,3,2,0:T(4,128)S(1)}, f32[3,3,3,3,128]{4,1,3,2,0:T(4,128)S(1)}, f32[3,3,3,3,128]{4,1,3,2,0:T(4,128)S(1)}, f32[...) while((s32[]{:T(128)}, f32[3,3,3,3,128]{4,1,3,2,0:T(4,128)S(1)}, ...), condition=%wide.region_94.95_spmd.clone, body=%wide.region_90.94_spmd.sunk.clone.sunk | while | flops 4269314 | bytes 2681977 | solution.py:46
  258.9 5.6 %while.457 = (s32[]{:T(128)}, f32[3,3,3,3,128]{4,1,3,2,0:T(4,128)S(1)}, f32[3,3,3,3,128]{4,1,3,2,0:T(4,128)S(1)}, f32[3,3,3,3,128]{4,1,3,2,0:T(4,128)S(1)}, f32[...) while((s32[]{:T(128)}, f32[3,3,3,3,128]{4,1,3,2,0:T(4,128)S(1)}, ...), condition=%wide.region_99.100_spmd.clone, body=%wide.region_95.0_spmd.sunk.clone.sunk | while | flops 4269314 | bytes 2681977 | solution.py:46
  259.7 1.1 fusion.291
  264.6 5.6 %while.459 = (s32[]{:T(128)}, f32[3,3,3,3,128]{4,1,3,2,0:T(4,128)S(1)}, f32[3,3,3,3,128]{4,1,3,2,0:T(4,128)S(1)}, f32[3,3,3,3,128]{4,1,3,2,0:T(4,128)S(1)}, f32[...) while((s32[]{:T(128)}, f32[3,3,3,3,128]{4,1,3,2,0:T(4,128)S(1)}, ...), condition=%wide.region_109.110_spmd.clone, body=%wide.region_105.109_spmd.sunk.clone.sunk | while | flops 4269314 | bytes 2681977 | solution.py:46
  270.2 5.6 %while.460 = (s32[]{:T(128)}, f32[3,3,3,3,128]{4,1,3,2,0:T(4,128)S(1)}, f32[3,3,3,3,128]{4,1,3,2,0:T(4,128)S(1)}, f32[3,3,3,3,128]{4,1,3,2,0:T(4,128)S(1)}, f32[...) while((s32[]{:T(128)}, f32[3,3,3,3,128]{4,1,3,2,0:T(4,128)S(1)}, ...), condition=%wide.region_114.115_spmd.clone, body=%wide.region_110.114_spmd.sunk.clone.sunk | while | flops 4269314 | bytes 2681977 | solution.py:46
  275.8 5.6 %while.462 = (s32[]{:T(128)}, f32[3,3,3,3,128]{4,1,3,2,0:T(4,128)S(1)}, f32[3,3,3,3,128]{4,1,3,2,0:T(4,128)S(1)}, f32[3,3,3,3,128]{4,1,3,2,0:T(4,128)S(1)}, f32[...) while((s32[]{:T(128)}, f32[3,3,3,3,128]{4,1,3,2,0:T(4,128)S(1)}, ...), condition=%wide.region_124.125_spmd.clone, body=%wide.region_120.124_spmd.sunk.clone.sunk | while | flops 4269314 | bytes 2681977 | solution.py:46
  281.4 5.6 %while.463 = (s32[]{:T(128)}, f32[3,3,3,3,128]{4,1,3,2,0:T(4,128)S(1)}, f32[3,3,3,3,128]{4,1,3,2,0:T(4,128)S(1)}, f32[3,3,3,3,128]{4,1,3,2,0:T(4,128)S(1)}, f32[...) while((s32[]{:T(128)}, f32[3,3,3,3,128]{4,1,3,2,0:T(4,128)S(1)}, ...), condition=%wide.region_129.130_spmd.clone, body=%wide.region_125.129_spmd.sunk.clone.sunk | while | flops 4269314 | bytes 2681977 | solution.py:46
  287.0 5.8 %while.465 = (s32[]{:T(128)}, f32[3,3,3,3,128]{4,1,3,2,0:T(4,128)S(1)}, f32[3,3,3,3,128]{4,1,3,2,0:T(4,128)S(1)}, f32[3,3,3,3,128]{4,1,3,2,0:T(4,128)S(1)}, f32[3,3,3,3,128]{4,1,3,2,0:T(4,128)S(1)}, /*index=5*/s32[]{:T(128)}) while((s32[]{:T(128)}, f32[3,3,3,3,128]{4,1,3,2,0:T(4,128)S(1)}, ...), condition=%wide.region_139.140_spmd.clone, body=%wide.region_135.139_spmd.sunk.clone.sunk | while | flops 4269314 | bytes 2681945 | solution.py:46
  288.0 1.1 fusion.299
  289.9 1.1 fusion.299
  291.7 1.1 fusion.299
  293.6 2.0 collective-permute-start.9
  302.2 11.0 %collective-permute-start.10 = (f32[3,4,1,3,128]{4,0,3,2,1:T(4,128)S(1)}, f32[3,4,1,3,128]{4,0,3,2,1:T(4,128)S(1)}, u32[]{:S(2)}, u32[]{:S(2)}) collective-permute-start(f32[3,4,1,3,128]{4,0,3,2,1:T(4,128)S(1)} %pad_maximum_fusion.7), channel_id=1, source_target_pairs={{56,0},{0,8},{8,16},{16,24},{24,32},{32,40},{40,48},{48,56},{57,1}... | collective-permute-start | bytes 55304 | tf_op jit(solution)/shard_map/ppermute | solution.py:23
  314.6 12.6 %collective-permute-done.10 = f32[3,4,1,3,128]{4,0,3,2,1:T(4,128)S(1)} collective-permute-done((f32[3,4,1,3,128]{4,0,3,2,1:T(4,128)S(1)}, f32[3,4,1,3,128]{4,0,3,2,1:T(4,128)S(1)}, u32[]{:S(2)}, u32[]{:S(2)}) %collective-permute-start.10) | collective-permute-done | bytes 18464 | tf_op jit(solution)/shard_map/ppermute | solution.py:23
  327.2 3.6 collective-permute-start.11
  330.9 10.9 %while.437 = (s32[]{:T(128)}, f32[3,3,3,3,128]{4,1,3,2,0:T(4,128)S(1)}, s32[3,2,3,3,128]{4,3,2,1,0:T(4,128)S(1)}, f32[3,3,3,128]{3,2,1,0:T(4,128)S(1)}, f32[3,3,...) while((s32[]{:T(128)}, f32[3,3,3,3,128]{4,1,3,2,0:T(4,128)S(1)}, ...), condition=%wide.region_141.142_spmd, body=%wide.region_140.141_spmd.sunk | while | flops 20799364 | bytes 281213 | solution.py:73
  341.8 6.5 %collective-permute-done.11 = f32[3,1,3,3,128]{4,0,3,2,1:T(4,128)S(1)} collective-permute-done((f32[3,1,3,3,128]{4,0,3,2,1:T(4,128)S(1)}, f32[3,1,3,3,128]{4,0,3,2,1:T(4,128)S(1)}, u32[]{:S(2)}, u32[]{:S(2)}) %collective-permute-start.11) | collective-permute-done | bytes 13856 | tf_op jit(solution)/shard_map/ppermute | solution.py:23
  348.4 11.4 %collective-permute-start.12 = (f32[6,2,3,3,128]{4,0,3,2,1:T(8,128)S(1)}, f32[6,2,3,3,128]{4,0,3,2,1:T(8,128)S(1)}, u32[]{:S(2)}, u32[]{:S(2)}) collective-permute-start(f32[6,2,3,3,128]{4,0,3,2,1:T(8,128)S(1)} %pad_maximum_fusion.4), channel_id=1, source_target_pairs={{64,0},{128,64},{192,128},{256,192},{320,256},{384,320},{448,384},... | collective-permute-start | bytes 165896 | tf_op jit(solution)/shard_map/ppermute | solution.py:23
  361.5 13.6 %collective-permute-start.13 = (f32[6,5,2,3,128]{4,0,3,2,1:T(8,128)S(1)}, f32[6,5,2,3,128]{4,0,3,2,1:T(8,128)S(1)}, u32[]{:S(2)}, u32[]{:S(2)}) collective-permute-start(f32[6,5,2,3,128]{4,0,3,2,1:T(8,128)S(1)} %slice.2528), channel_id=1, source_target_pairs={{8,0},{16,8},{24,16},{32,24},{40,32},{48,40},{56,48},{0,56},{9,1},... | collective-permute-start | bytes 276488 | tf_op jit(solution)/shard_map/ppermute | solution.py:23
  375.1 14.3 %collective-permute-done.13 = f32[6,5,2,3,128]{4,0,3,2,1:T(8,128)S(1)} collective-permute-done((f32[6,5,2,3,128]{4,0,3,2,1:T(8,128)S(1)}, f32[6,5,2,3,128]{4,0,3,2,1:T(8,128)S(1)}, u32[]{:S(2)}, u32[]{:S(2)}) %collective-permute-start.13) | collective-permute-done | bytes 92192 | tf_op jit(solution)/shard_map/ppermute | solution.py:23
  392.1 4.0 collective-permute-done.14
  (1103 shorter events, 169.7 us)
Async XLA Ops:
  2.3 43.5 %collective-permute-start = (f32[3,1,3,3,128]{4,0,3,2,1:T(4,128)S(1)}, f32[3,1,3,3,128]{4,0,3,2,1:T(4,128)S(1)}, u32[]{:S(2)}, u32[]{:S(2)}) collective-permute-start(f32[3,1,3,3,128]{4,0,3,2,1:T(4,128)S(1)} %slice.2454), channel_id=1, source_target_pairs={{64,0},{128,64},{192,128},{256,192},{320,256},{384,320},{448,384},... | collective-permute-start | bytes 41480 | tf_op jit(solution)/shard_map/ppermute | solution.py:23
  40.1 5.4 %copy-start.14 = (s32[16,8,8]{0,2,1:T(8,128)S(1)}, s32[16,8,8]{0,2,1:T(8,128)}, u32[]{:S(2)}) copy-start(s32[16,8,8]{0,2,1:T(8,128)} %param.209) | copy-start | bytes 12292
  45.5 14.6 %copy-start.12 = (f32[3]{0:T(128)S(1)}, f32[3]{0:T(128)}, u32[]{:S(2)}) copy-start(f32[3]{0:T(128)} %constant.2148) | copy-start | bytes 40
  45.8 23.2 %collective-permute-start.1 = (f32[3,4,1,3,128]{4,0,3,2,1:T(4,128)S(1)}, f32[3,4,1,3,128]{4,0,3,2,1:T(4,128)S(1)}, u32[]{:S(2)}, u32[]{:S(2)}) collective-permute-start(f32[3,4,1,3,128]{4,0,3,2,1:T(4,128)S(1)} %pad_maximum_fusion.10), channel_id=1, source_target_pairs={{8,0},{16,8},{24,16},{32,24},{40,32},{48,40},{56,48},{0,56},{9,1},... | collective-permute-start | bytes 55304 | tf_op jit(solution)/shard_map/ppermute | solution.py:23
  65.7 5.3 %copy-start.11 = (f32[3]{0:T(128)S(1)}, f32[3]{0:T(128)}, u32[]{:S(2)}) copy-start(f32[3]{0:T(128)} %constant.2130) | copy-start | bytes 40
  69.0 18.8 %collective-permute-start.2 = (f32[3,4,4,1,128]{4,0,3,2,1:T(4,128)S(1)}, f32[3,4,4,1,128]{4,0,3,2,1:T(4,128)S(1)}, u32[]{:S(2)}, u32[]{:S(2)}) collective-permute-start(f32[3,4,4,1,128]{4,0,3,2,1:T(4,128)S(1)} %slice.2455), channel_id=1, source_target_pairs={{1,0},{2,1},{3,2},{4,3},{5,4},{6,5},{7,6},{0,7},{9,8},{10,9},{11,1... | collective-permute-start | bytes 73736 | tf_op jit(solution)/shard_map/ppermute | solution.py:23
  71.0 5.6 %copy-start.10 = (f32[3]{0:T(128)S(1)}, f32[3]{0:T(128)}, u32[]{:S(2)}) copy-start(f32[3]{0:T(128)} %constant.2139) | copy-start | bytes 40
  76.6 5.6 %copy-start.9 = (f32[3]{0:T(128)S(1)}, f32[3]{0:T(128)}, u32[]{:S(2)}) copy-start(f32[3]{0:T(128)} %constant.2157) | copy-start | bytes 40
  87.8 0.7 copy-start.8
  88.5 5.6 %copy-start.7 = (f32[3]{0:T(128)S(1)}, f32[3]{0:T(128)}, u32[]{:S(2)}) copy-start(f32[3]{0:T(128)} %constant.2127) | copy-start | bytes 40
  94.1 5.6 %copy-start.6 = (f32[3]{0:T(128)S(1)}, f32[3]{0:T(128)}, u32[]{:S(2)}) copy-start(f32[3]{0:T(128)} %constant.2133) | copy-start | bytes 40
  105.8 0.7 copy-start.5
  106.5 5.6 %copy-start.4 = (f32[3]{0:T(128)S(1)}, f32[3]{0:T(128)}, u32[]{:S(2)}) copy-start(f32[3]{0:T(128)} %constant.2142) | copy-start | bytes 40
  112.1 5.6 %copy-start.3 = (f32[3]{0:T(128)S(1)}, f32[3]{0:T(128)}, u32[]{:S(2)}) copy-start(f32[3]{0:T(128)} %constant.2145) | copy-start | bytes 40
  117.7 5.6 %copy-start.2 = (f32[3]{0:T(128)S(1)}, f32[3]{0:T(128)}, u32[]{:S(2)}) copy-start(f32[3]{0:T(128)} %constant.2151) | copy-start | bytes 40
  123.4 5.6 %copy-start.1 = (f32[3]{0:T(128)S(1)}, f32[3]{0:T(128)}, u32[]{:S(2)}) copy-start(f32[3]{0:T(128)} %constant.2154) | copy-start | bytes 40
  141.0 14.6 %copy-start.15 = (s32[16,8]{0,1:T(8,128)S(1)}, s32[16,8]{0,1:T(8,128)}, u32[]{:S(2)}) copy-start(s32[16,8]{0,1:T(8,128)} %param.208) | copy-start | bytes 1540
  141.1 48.1 %copy-start = (f32[3,3,3,3,128]{4,3,2,1,0:T(4,128)S(1)}, f32[3,3,3,3,128]{4,3,2,1,0:T(4,128)}, u32[]{:S(2)}) copy-start(f32[3,3,3,3,128]{4,3,2,1,0:T(4,128)} %param.203) | copy-start | bytes 124420
  141.1 48.1 %copy-start.13 = (f32[3,3,3,3,128]{4,3,2,1,0:T(4,128)S(1)}, f32[3,3,3,3,128]{4,3,2,1,0:T(4,128)}, u32[]{:S(2)}) copy-start(f32[3,3,3,3,128]{4,3,2,1,0:T(4,128)} %param.204) | copy-start | bytes 124420
  141.2 2.1 collective-permute-start.3
  143.3 25.1 %collective-permute-start.4 = (f32[3,4,1,3,128]{4,0,3,2,1:T(4,128)S(1)}, f32[3,4,1,3,128]{4,0,3,2,1:T(4,128)S(1)}, u32[]{:S(2)}, u32[]{:S(2)}) collective-permute-start(f32[3,4,1,3,128]{4,0,3,2,1:T(4,128)S(1)} %pad_maximum_fusion.9), channel_id=1, source_target_pairs={{56,0},{0,8},{8,16},{16,24},{24,32},{32,40},{40,48},{48,56},{57,1}... | collective-permute-start | bytes 55304 | tf_op jit(solution)/shard_map/ppermute | solution.py:23
  168.5 20.7 %collective-permute-start.5 = (f32[3,1,3,3,128]{4,0,3,2,1:T(4,128)S(1)}, f32[3,1,3,3,128]{4,0,3,2,1:T(4,128)S(1)}, u32[]{:S(2)}, u32[]{:S(2)}) collective-permute-start(f32[3,1,3,3,128]{4,0,3,2,1:T(4,128)S(1)} %slice.2489), channel_id=1, source_target_pairs={{960,0},{0,64},{64,128},{128,192},{192,256},{256,320},{320,384},{3... | collective-permute-start | bytes 41480 | tf_op jit(solution)/shard_map/ppermute | solution.py:23
  189.3 7.3 %collective-permute-start.6 = (f32[3,1,3,3,128]{4,0,3,2,1:T(4,128)S(1)}, f32[3,1,3,3,128]{4,0,3,2,1:T(4,128)S(1)}, u32[]{:S(2)}, u32[]{:S(2)}) collective-permute-start(f32[3,1,3,3,128]{4,0,3,2,1:T(4,128)S(1)} %slice.2491), channel_id=1, source_target_pairs={{64,0},{128,64},{192,128},{256,192},{320,256},{384,320},{448,384},... | collective-permute-start | bytes 41480 | tf_op jit(solution)/shard_map/ppermute | solution.py:23
  196.7 22.9 %collective-permute-start.7 = (f32[3,4,1,3,128]{4,0,3,2,1:T(4,128)S(1)}, f32[3,4,1,3,128]{4,0,3,2,1:T(4,128)S(1)}, u32[]{:S(2)}, u32[]{:S(2)}) collective-permute-start(f32[3,4,1,3,128]{4,0,3,2,1:T(4,128)S(1)} %pad_maximum_fusion.8), channel_id=1, source_target_pairs={{8,0},{16,8},{24,16},{32,24},{40,32},{48,40},{56,48},{0,56},{9,1},... | collective-permute-start | bytes 55304 | tf_op jit(solution)/shard_map/ppermute | solution.py:23
  219.6 21.8 %collective-permute-start.8 = (f32[3,4,4,1,128]{4,0,3,2,1:T(4,128)S(1)}, f32[3,4,4,1,128]{4,0,3,2,1:T(4,128)S(1)}, u32[]{:S(2)}, u32[]{:S(2)}) collective-permute-start(f32[3,4,4,1,128]{4,0,3,2,1:T(4,128)S(1)} %slice.2492), channel_id=1, source_target_pairs={{1,0},{2,1},{3,2},{4,3},{5,4},{6,5},{7,6},{0,7},{9,8},{10,9},{11,1... | collective-permute-start | bytes 73736 | tf_op jit(solution)/shard_map/ppermute | solution.py:23
  293.3 2.3 copy-start.16
  293.6 8.5 %collective-permute-start.9 = (f32[3,4,4,1,128]{4,0,3,2,1:T(4,128)S(1)}, f32[3,4,4,1,128]{4,0,3,2,1:T(4,128)S(1)}, u32[]{:S(2)}, u32[]{:S(2)}) collective-permute-start(f32[3,4,4,1,128]{4,0,3,2,1:T(4,128)S(1)} %slice.2523), channel_id=1, source_target_pairs={{7,0},{0,1},{1,2},{2,3},{3,4},{4,5},{5,6},{6,7},{15,8},{8,9},{9,10... | collective-permute-start | bytes 73736 | tf_op jit(solution)/shard_map/ppermute | solution.py:23
  302.2 25.0 %collective-permute-start.10 = (f32[3,4,1,3,128]{4,0,3,2,1:T(4,128)S(1)}, f32[3,4,1,3,128]{4,0,3,2,1:T(4,128)S(1)}, u32[]{:S(2)}, u32[]{:S(2)}) collective-permute-start(f32[3,4,1,3,128]{4,0,3,2,1:T(4,128)S(1)} %pad_maximum_fusion.7), channel_id=1, source_target_pairs={{56,0},{0,8},{8,16},{16,24},{24,32},{32,40},{40,48},{48,56},{57,1}... | collective-permute-start | bytes 55304 | tf_op jit(solution)/shard_map/ppermute | solution.py:23
  327.2 21.1 %collective-permute-start.11 = (f32[3,1,3,3,128]{4,0,3,2,1:T(4,128)S(1)}, f32[3,1,3,3,128]{4,0,3,2,1:T(4,128)S(1)}, u32[]{:S(2)}, u32[]{:S(2)}) collective-permute-start(f32[3,1,3,3,128]{4,0,3,2,1:T(4,128)S(1)} %slice.2526), channel_id=1, source_target_pairs={{960,0},{0,64},{64,128},{128,192},{192,256},{256,320},{320,384},{3... | collective-permute-start | bytes 41480 | tf_op jit(solution)/shard_map/ppermute | solution.py:23
  348.4 13.0 %collective-permute-start.12 = (f32[6,2,3,3,128]{4,0,3,2,1:T(8,128)S(1)}, f32[6,2,3,3,128]{4,0,3,2,1:T(8,128)S(1)}, u32[]{:S(2)}, u32[]{:S(2)}) collective-permute-start(f32[6,2,3,3,128]{4,0,3,2,1:T(8,128)S(1)} %pad_maximum_fusion.4), channel_id=1, source_target_pairs={{64,0},{128,64},{192,128},{256,192},{320,256},{384,320},{448,384},... | collective-permute-start | bytes 165896 | tf_op jit(solution)/shard_map/ppermute | solution.py:23
  361.5 27.9 %collective-permute-start.13 = (f32[6,5,2,3,128]{4,0,3,2,1:T(8,128)S(1)}, f32[6,5,2,3,128]{4,0,3,2,1:T(8,128)S(1)}, u32[]{:S(2)}, u32[]{:S(2)}) collective-permute-start(f32[6,5,2,3,128]{4,0,3,2,1:T(8,128)S(1)} %slice.2528), channel_id=1, source_target_pairs={{8,0},{16,8},{24,16},{32,24},{40,32},{48,40},{56,48},{0,56},{9,1},... | collective-permute-start | bytes 276488 | tf_op jit(solution)/shard_map/ppermute | solution.py:23
  389.6 6.4 %collective-permute-start.14 = (f32[6,5,5,2,128]{4,0,3,2,1:T(8,128)S(1)}, f32[6,5,5,2,128]{4,0,3,2,1:T(8,128)S(1)}, u32[]{:S(2)}, u32[]{:S(2)}) collective-permute-start(f32[6,5,5,2,128]{4,0,3,2,1:T(8,128)S(1)} %slice.2529), channel_id=1, source_target_pairs={{1,0},{2,1},{3,2},{4,3},{5,4},{6,5},{7,6},{0,7},{9,8},{10,9},{11,1... | collective-permute-start | bytes 460808 | tf_op jit(solution)/shard_map/ppermute | solution.py:23
where the time goes:
time: 403 us; the launch traced here: 397 us
  other arithmetic  149 us (37%)
  starting transfers between devices  120 us (30%)
  waiting for transfers between devices  76.1 us (19%)
  matrix products  21 us (5%)
  between operations  12.2 us (3%)
  local copies, waits for them, and re-layouts  10.5 us (3%)
  loops' own time  8.01 us (2%)
    ppermute x15, starting transfers between devices, from_behind(): return lax.ppermute(block, axis, route)  120 us
    reduce_sum x78, other arithmetic, pair_one_plane(): jnp.sum(pushes, axis=2).reshape(pieces[0].shape)  83.4 us
    ppermute x15, waiting for transfers between devices, from_behind(): return lax.ppermute(block, axis, route)  76.1 us
    reduce_sum x84, other arithmetic, pair_term(): distance = jnp.sum(separation * separation, axis=0)  44.3 us
    mul x84, other arithmetic, pair_term(): return (STRENGTH * jnp.exp(-distance / SPREAD))[None] * separation  9.15 us
  transfers between devices with their start and end apart: 15, of which 10 were waited for; matrix products, arithmetic and copies ran while one was open for 20% of the time, Pallas kernels for 0%

commit v1 on v0

v1 whole, which is shorter than its diff:
```python
import functools
import math

import jax
import jax.numpy as jnp
from jax import lax
from jax.experimental import pallas as pl
from jax.experimental.pallas import tpu as pltpu
from jax.sharding import PartitionSpec as P

STRENGTH = 0.3
SPREAD = 0.6
STEP_DT = 0.2
F32 = jnp.float32
BF16 = jnp.bfloat16
SCALE = math.sqrt(1.0 / (SPREAD * math.log(2.0)))
PUSH = STRENGTH / SCALE
DEAD = -1.0e6
N = 128
V = pl.BlockSpec(memory_space=pltpu.VMEM)
S = pl.BlockSpec(memory_space=pltpu.SMEM)


def call(kernel, name, ins, outs, scratch=(), specs=None, to_hbm=False):
    specs = [V] * len(ins) if specs is None else specs
    return pl.pallas_call(
        kernel,
        name=name,
        out_shape=[
            (jax.ShapeDtypeStruct if to_hbm else pltpu.VMEM)(shape, F32) for shape in outs
        ],
        in_specs=specs,
        out_specs=[V] * len(outs),
        scratch_shapes=list(scratch),
    )(*[
        pltpu.with_memory_space_constraint(value, pltpu.VMEM) if spec is V else value
        for value, spec in zip(ins, specs)
    ])


def living_row(count):
    return (lax.broadcasted_iota(jnp.int32, (1, N), 1) < count).astype(F32)


def pack_first(pos, counts, own, top, bottom):
    for z in range(3):
        for y in range(3):
            for x in range(3):
                rows = [pos[k, z, y, x : x + 1, :] for k in range(3)]
                cell = jnp.concatenate(rows + [living_row(counts[z, y, x])], axis=0)
                own[9 * z + 3 * y + x] = cell
                if z == 2:
                    top[3 * y + x] = cell
                if z == 0:
                    bottom[3 * y + x] = cell


SWAP_CELLS = [
    (p, y, x)
    for p in range(-1, 4)
    for y in (range(3) if p in (-1, 3) else (0, 2))
    for x in range(3)
]
SWAP_AT = {cell: at for at, cell in enumerate(SWAP_CELLS)}


def pack_swap(own, low, high, out):
    for (p, y, x), at in SWAP_AT.items():
        if p == -1:
            out[at] = low[3 * y + x]
        elif p == 3:
            out[at] = high[3 * y + x]
        else:
            out[at] = own[9 * p + 3 * y + x]


def even_column():
    return lax.axis_index("gy") % 2 == 0


def lowest_plane():
    return lax.axis_index("gz") == 0


def highest_plane():
    return lax.axis_index("gz") == 15


def partner_cell(low, high, swapped, p, y, x):
    there = swapped[SWAP_AT[p, y, x]]
    if p == -1:
        return jnp.where(lowest_plane(), low[3 * y + x], there)
    if p == 3:
        return jnp.where(highest_plane(), high[3 * y + x], there)
    return there


def own_cell(own, low, high, swapped, p, y, x):
    if p == -1:
        return jnp.where(lowest_plane(), swapped[SWAP_AT[p, y, x]], low[3 * y + x])
    if p == 3:
        return jnp.where(highest_plane(), swapped[SWAP_AT[p, y, x]], high[3 * y + x])
    return own[9 * p + 3 * y + x]


def pack_relay(low, high, swapped, out):
    even = even_column()
    for p in range(-1, 4):
        for x in range(3):
            upper = partner_cell(low, high, swapped, p, 2, x)
            lower = partner_cell(low, high, swapped, p, 0, x)
            out[3 * (p + 1) + x] = jnp.where(even, upper, lower)


def pack_middle(own, low, high, swapped, relayed, middle, left, right):
    even = even_column()
    for p in range(-1, 4):
        for y in range(-1, 4):
            for x in range(3):
                if y in (-1, 3):
                    near = partner_cell(low, high, swapped, p, 2 if y == -1 else 0, x)
                    far = relayed[3 * (p + 1) + x]
                    if y == -1:
                        near, far = far, near
                    cell = jnp.where(even, near, far)
                else:
                    cell = own_cell(own, low, high, swapped, p, y, x)
                row = 5 * (p + 1) + y + 1
                middle[3 * row + x] = cell
                if x == 0:
                    left[row] = cell
                if x == 2:
                    right[row] = cell


def three(x):
    first = x.astype(BF16).astype(F32)
    rest = x - first
    second = rest.astype(BF16).astype(F32)
    return first, second, rest - second


def scaled_cell(cell, p, y, x):
    alive = cell[3:4] > 0.5
    at = lax.broadcasted_iota(jnp.int32, (3, 1), 0)
    shift = jnp.where(at == 0, p, jnp.where(at == 1, y, x)).astype(F32) - 1.5
    return jnp.where(alive, (cell[0:3] + shift) * SCALE, 0.0), alive


def partner_rows(coords, alive):
    norm = jnp.where(alive, -jnp.sum(coords * coords, axis=0, keepdims=True), DEAD)
    b1, b2, b3 = three(jnp.concatenate([coords, norm], axis=0))
    ones = jnp.concatenate([jnp.ones((3, N), F32), jnp.zeros((1, N), F32)], axis=0)
    zeros = jnp.zeros((4, N), F32)
    return jnp.concatenate([zeros, b1, b1, b2, b1, b2, b3, ones], axis=0)


def own_rows(coords):
    norm = -jnp.sum(coords * coords, axis=0, keepdims=True)
    a1, a2, a3 = three(jnp.concatenate([2.0 * coords, jnp.ones((1, N), F32)], axis=0))
    zeros = jnp.zeros((1, N), F32)
    tail = jnp.concatenate(list(three(norm)) + [zeros], axis=0)
    return jnp.concatenate([jnp.zeros((4, N), F32), a1, a2, a1, a3, a2, a1, tail], axis=0)


def product(left, right, right_turned=False):
    dims = (((1,), (1 if right_turned else 0,)), ((), ()))
    return lax.dot_general(left, right, dims, preferred_element_type=F32)


def store_operands(rows, at, b_ref, x_ref):
    b_ref[at] = rows.T.astype(BF16)
    x_ref[at] = rows[16:32].astype(BF16)


AHEAD = 8


def push_rows(acc_ref, blocks, b_ref, x_ref, a_ref):
    def reach(block):
        return max(0, block[1] - 1), min(2, block[1] + 1) + 1

    def exponents(block):
        first, last = reach(block)
        return product(b_ref[block[2]], a_ref[block[0], :, N * first : N * last])

    waiting = [exponents(block) for block in blocks[:AHEAD]]
    sums = [None, None, None]
    for at, block in enumerate(blocks):
        if at + AHEAD < len(blocks):
            waiting.append(exponents(blocks[at + AHEAD]))
        weight = jnp.exp2(waiting.pop(0))
        high = weight.astype(BF16)
        low = (weight - high.astype(F32)).astype(BF16)
        x_op = x_ref[block[2]]
        value = product(
            jnp.concatenate([x_op, x_op], axis=1), jnp.concatenate([high, low], axis=0)
        )
        first, last = reach(block)
        for x in range(first, last):
            part = value[:, N * (x - first) : N * (x - first + 1)]
            sums[x] = part if sums[x] is None else sums[x] + part
        if at + 1 == len(blocks) or blocks[at + 1][3] != block[3]:
            for x in range(3):
                if sums[x] is not None:
                    acc_ref[3 * block[0] + x] += sums[x]
            sums = [None, None, None]


def cell_force(acc, coords):
    total = acc[0:4] + acc[4:8] + acc[8:12]
    return PUSH * (coords * acc[12:15] - total[0:3])


def z_pair(step):
    z = (step + 1) // 3
    return z, step - 2 * z


def own_pairs(own, counts, bonds, acc_out, bond_out, b_ref, x_ref, a_ref):
    def prepare(row, _):
        z, y = row // 3, row % 3
        for x in range(3):
            coords, alive = scaled_cell(own[3 * row + x], z, y, x)
            store_operands(partner_rows(coords, alive), 3 * row + x, b_ref, x_ref)
            a_ref[row, :, N * x : N * (x + 1)] = own_rows(coords).astype(BF16)
            acc_out[3 * row + x] = jnp.zeros((16, N), F32)
            bond_out[3 * row + x] = bond_cell(
                own[3 * row + x], bonds[z, y, x, 0:1], bonds[z, y, x, 1:2], counts[z, y, x],
            )
        return 0

    lax.fori_loop(0, 9, prepare, 0)

    def sweep(step, _):
        z, other = z_pair(step)
        blocks = [
            (3 * z + y, x, 9 * other + 3 * near + x, y)
            for y in range(3)
            for near in range(max(0, y - 1), min(2, y + 1) + 1)
            for x in range(3)
        ]
        push_rows(acc_out, blocks, b_ref, x_ref, a_ref)
        return 0

    lax.fori_loop(0, 7, sweep, 0)


def bond_cell(cell, heads, tails, count):
    place = lax.broadcasted_iota(jnp.int32, (N, N), 0)
    pick = (place == tails).astype(F32) - (place == heads).astype(F32)
    pick = pick.astype(BF16)
    both = ((heads < count) & (tails < count)).astype(F32)
    zeros = jnp.zeros((4, N), F32)
    split = jnp.concatenate(list(three(cell)) + [zeros], axis=0).astype(BF16)
    found = product(split, pick)
    tension = both * (found[0:4] + found[4:8] + found[8:12])
    split = jnp.concatenate(list(three(tension)) + [zeros], axis=0).astype(BF16)
    back = product(split, pick, True)
    return -(back[0:4] + back[4:8] + back[8:12])


def other_pairs(middle, left, right, acc_in, acc, b_ref, x_ref, a_ref):
    def prepare(row, _):
        p, y = row // 5 - 1, row % 5 - 1
        for x in range(-1, 4):
            cell = left[row] if x == -1 else right[row] if x == 3 else middle[3 * row + x]
            coords, alive = scaled_cell(cell, p, y, x)
            store_operands(partner_rows(coords, alive), 5 * row + x + 1, b_ref, x_ref)
        return 0

    lax.fori_loop(0, 25, prepare, 0)

    def prepare_own(row, _):
        z, y = row // 3, row % 3
        for x in range(3):
            cell = middle[3 * (5 * (z + 1) + y + 1) + x]
            coords, alive = scaled_cell(cell, z, y, x)
            a_ref[row, :, N * x : N * (x + 1)] = own_rows(coords).astype(BF16)
            acc[3 * row + x] = acc_in[3 * row + x]
        return 0

    lax.fori_loop(0, 9, prepare_own, 0)

    def row_blocks(row, at_row, columns, tag):
        return [(row, x, 5 * at_row + x + 1, tag) for x in columns]

    def within(step, _):
        z, other = z_pair(step)
        blocks = []
        for y in range(3):
            for near in range(y - 1, y + 2):
                columns = (-1, 3) if 0 <= near <= 2 else range(-1, 4)
                blocks += row_blocks(3 * z + y, 5 * (other + 1) + near + 1, columns, y)
        push_rows(acc, blocks, b_ref, x_ref, a_ref)
        return 0

    lax.fori_loop(0, 7, within, 0)

    def across(step, _):
        side, y = step // 3, step % 3
        blocks = []
        for near in range(-1, 2):
            blocks += row_blocks(6 * side + y, 20 * side + y + near + 1, range(-1, 4), 0)
        push_rows(acc, blocks, b_ref, x_ref, a_ref)
        return 0

    lax.fori_loop(0, 6, across, 0)


def step_one(
    middle, left, right, acc_in, bond, vel, forces, own, top, bottom, acc, b_ref, x_ref, a_ref
):
    other_pairs(middle, left, right, acc_in, acc, b_ref, x_ref, a_ref)
    for z in range(3):
        for y in range(3):
            for x in range(3):
                at = 9 * z + 3 * y + x
                cell = middle[3 * (5 * (z + 1) + y + 1) + x]
                coords, _ = scaled_cell(cell, z, y, x)
                force = (cell_force(acc[at], coords) + bond[at][0:3]) * cell[3:4]
                speed = jnp.concatenate([vel[k, z, y, x : x + 1, :] for k in range(3)], axis=0)
                moved = cell[0:3] + STEP_DT * speed + 0.5 * STEP_DT * STEP_DT * force
                fresh = jnp.concatenate([moved, cell[3:4]], axis=0)
                own[at] = fresh
                if z == 2:
                    top[at - 18] = fresh
                if z == 0:
                    bottom[at] = fresh
                for k in range(3):
                    forces[k, z, y, x : x + 1, :] = force[k : k + 1]


def step_two(middle, left, right, acc_in, bond, carried, bottom, acc, b_ref, x_ref, a_ref):
    other_pairs(middle, left, right, acc_in, acc, b_ref, x_ref, a_ref)
    for z in range(3):
        for y in range(3):
            for x in range(3):
                at = 9 * z + 3 * y + x
                cell = middle[3 * (5 * (z + 1) + y + 1) + x]
                coords, _ = scaled_cell(cell, z, y, x)
                force = (cell_force(acc[at], coords) + bond[at][0:3]) * cell[3:4]
                both = jnp.concatenate([cell[0:3] * cell[3:4], force], axis=0)
                carried[at] = both
                if z < 2:
                    bottom[6 * at : 6 * at + 6] = both


HAND_CELLS = [
    (p, y, x) for p in range(5) for y in range(2 if p < 3 else 3) for x in range(3)
]
HAND_AT = {cell: at for at, cell in enumerate(HAND_CELLS)}


def rows6(ref, at):
    return ref[6 * at : 6 * at + 6]


def pack_hand(own, high, out):
    for (p, y, x), at in HAND_AT.items():
        value = own[9 * p + 3 * y + x] if p < 3 else rows6(high, 9 * (p - 3) + 3 * y + x)
        out[6 * at : 6 * at + 6] = value


def partner_six(high, swapped, p, y, x):
    there = rows6(swapped, HAND_AT[p, y, x])
    if p < 3:
        return there
    return jnp.where(highest_plane(), rows6(high, 9 * (p - 3) + 3 * y + x), there)


def pack_hand_relay(high, swapped, out):
    for p in range(5):
        for y in range(2):
            for x in range(3):
                at = 6 * p + 3 * y + x
                out[6 * at : 6 * at + 6] = partner_six(high, swapped, p, y, x)


def pack_hand_side(own, high, swapped, relayed, middle, side):
    even = even_column()
    for p in range(5):
        for y in range(5):
            for x in range(3):
                if y >= 3:
                    near = partner_six(high, swapped, p, y - 3, x)
                    far = rows6(relayed, 6 * p + 3 * (y - 3) + x)
                    value = jnp.where(even, near, far)
                elif p < 3:
                    value = own[9 * p + 3 * y + x]
                else:
                    near = rows6(high, 9 * (p - 3) + 3 * y + x)
                    far = rows6(swapped, HAND_AT[p, y, x])
                    value = jnp.where(highest_plane(), far, near)
                middle[15 * p + 3 * y + x] = value
                if x < 2:
                    at = 10 * p + 2 * y + x
                    side[6 * at : 6 * at + 6] = value


def place(plan_z, plan_y, plan_x, middle, side, moved, forces, ext):
    i, j, k = (lax.axis_index(name) for name in ("gz", "gy", "gx"))
    lows = (plan_z[(i + 15) % 16], plan_y[(j + 7) % 8, i], plan_x[j, (k + 7) % 8, i])
    fills = [
        3 + up - low for up, low in zip((plan_z[i], plan_y[j, i], plan_x[j, k, i]), lows)
    ]
    for row in range(25):
        for x in range(3):
            ext[5 * row + x, 0:6] = middle[3 * row + x]
        for x in range(2):
            ext[5 * row + 3 + x, 0:6] = rows6(side, 2 * row + x)

    def plane(s, _):
        z = jnp.minimum(lows[0] + s, 4)
        for t in range(5):
            y = jnp.minimum(lows[1] + t, 4)
            for u in range(5):
                x = jnp.minimum(lows[2] + u, 4)
                used = (s < fills[0]) & (t < fills[1]) & (u < fills[2])
                value = jnp.where(used, ext[25 * z + 5 * y + x], 0.0)
                moved[s, t, u] = value[0:3]
                forces[s, t, u] = value[3:6]
        return 0

    lax.fori_loop(0, 5, plane, 0)


def gz_gy(z, y):
    return (z % 16) * 8 + 2 * y + z // 16


def z_ring(block, distance):
    route = [
        (gz_gy((z - distance) % 32, y), gz_gy(z, y)) for z in range(32) for y in range(4)
    ]
    return lax.ppermute(block, ("gz", "gy"), route)


def swap(block):
    return lax.ppermute(block, "gy", [(i ^ 1, i) for i in range(8)])


def relay(block, up_to_odd_only=False):
    pairs = [((i - 2 if i % 2 == 0 else i + 2) % 8, i) for i in range(8)]
    if up_to_odd_only:
        pairs = [pair for pair in pairs if pair[1] % 2 == 1]
    return lax.ppermute(block, "gy", pairs)


def along_x(block, distance):
    return lax.ppermute(block, "gx", [((i - distance) % 8, i) for i in range(8)])


def halo_and_own(own, top, bottom, counts, bonds):
    low = z_ring(top, 1)
    high = z_ring(bottom, -1)
    (message,) = call(pack_swap, "pack_swap", (own, low, high), [(36, 4, N)])
    swapped = swap(message)
    acc, bond = call(
        own_pairs, "own_pairs", (own, counts, bonds), [(27, 16, N), (27, 4, N)],
        [pltpu.VMEM((27, N, 32), BF16), pltpu.VMEM((27, 16, N), BF16),
         pltpu.VMEM((9, 32, 3 * N), BF16)],
        [V, S, V],
    )
    (message,) = call(
        pack_relay, "pack_relay", (low, high, swapped), [(15, 4, N)]
    )
    relayed = relay(message)
    middle, left, right = call(
        pack_middle, "pack_middle", (own, low, high, swapped, relayed),
        [(75, 4, N), (25, 4, N), (25, 4, N)],
    )
    return middle, along_x(right, 1), along_x(left, -1), acc, bond


PAIR_SCRATCH = [
    pltpu.VMEM((27, 16, N), F32), pltpu.VMEM((125, N, 32), BF16),
    pltpu.VMEM((125, 16, N), BF16), pltpu.VMEM((9, 32, 3 * N), BF16),
]


def on_device(positions, velocities, counts, bonds, plan_z, plan_y, plan_x):
    bonds = jnp.moveaxis(bonds, 0, 3)
    own, top, bottom = call(
        pack_first, "pack_first", (positions, counts), [(27, 4, N), (9, 4, N), (9, 4, N)], (),
        [V, S],
    )
    middle, left, right, acc, bond = halo_and_own(own, top, bottom, counts, bonds)
    forces_first, own, top, bottom = call(
        step_one, "step_one", (middle, left, right, acc, bond, velocities),
        [(3, 3, 3, 3, N), (27, 4, N), (9, 4, N), (9, 4, N)], PAIR_SCRATCH,
    )
    middle, left, right, acc, bond = halo_and_own(own, top, bottom, counts, bonds)
    own, bottom = call(
        step_two, "step_two", (middle, left, right, acc, bond), [(27, 6, N), (108, N)],
        PAIR_SCRATCH,
    )
    high = z_ring(bottom, -1)
    (message,) = call(pack_hand, "pack_hand", (own, high), [(216, N)])
    swapped = swap(message)
    (message,) = call(
        pack_hand_relay, "pack_hand_relay", (high, swapped), [(180, N)]
    )
    relayed = relay(message, True)
    middle, side = call(
        pack_hand_side, "pack_hand_side", (own, high, swapped, relayed),
        [(75, 6, N), (300, N)],
    )
    side = along_x(side, -1)
    moved_positions, moved_forces = call(
        place, "place", (plan_z, plan_y.T, plan_x.transpose(1, 2, 0), middle, side),
        [(5, 5, 5, 3, N), (5, 5, 5, 3, N)], [pltpu.VMEM((125, 8, N), F32)], [S, S, S, V, V],
        to_hbm=True,
    )
    return forces_first, jnp.moveaxis(moved_positions, 3, 0), jnp.moveaxis(moved_forces, 3, 0)


def solution(mesh):
    bricks = P(None, "gz", "gy", "gx", None)
    return jax.shard_map(
        on_device,
        mesh=mesh,
        in_specs=(bricks, bricks, P("gz", "gy", "gx"), bricks, P(), P(), P()),
        out_specs=(bricks, bricks, bricks),
        check_vma=False,
    )
```

time: 403 us -> 213 us (0.53)
  the two profiles are of different devices: /device:TPU:7 before, /device:TPU:31 now
where the time goes in v1:
time: 213 us; the launch traced here: 212 us
  starting transfers between devices  110 us (52%)
  Pallas kernels  50.7 us (24%)
  waiting for transfers between devices  49.7 us (23%)
    ppermute x3, starting transfers between devices, swap(): return lax.ppermute(block, 'gy', [(i ^ 1, i) for i in range(8)])  52.2 us
    pallas_call x15, Pallas kernels, call(): pl.pallas_call(kernel, name=name, out_shape=[(jax.ShapeDtypeStruct if to_...  50.7 us
    ppermute x5, starting transfers between devices, z_ring(): return lax.ppermute(block, ('gz', 'gy'), route)  41.5 us
    ppermute x3, waiting for transfers between devices, swap(): return lax.ppermute(block, 'gy', [(i ^ 1, i) for i in range(8)])  21 us
    ppermute x5, waiting for transfers between devices, along_x(): lax.ppermute(block, 'gx', [((i - distance) % 8, i) for i in range(8)])  20.3 us
    ppermute x5, starting transfers between devices, along_x(): lax.ppermute(block, 'gx', [((i - distance) % 8, i) for i in range(8)])  11.3 us
    ppermute x3, waiting for transfers between devices, relay(): return lax.ppermute(block, 'gy', pairs)  5.42 us
    ppermute x3, starting transfers between devices, relay(): return lax.ppermute(block, 'gy', pairs)  4.51 us
  transfers between devices with their start and end apart: 16, of which 9 were waited for; matrix products, arithmetic and copies ran while one was open for 0% of the time, Pallas kernels for 10%

profile of v1, /device:TPU:31, one launch (start us, length us, event | category | flops | bytes accessed | tf_op | source)
XLA Modules:
  0.0 212.3 jit_solution(6257596062297261461)
XLA Ops:
  0.6 0.0 copy-start.2
  0.6 0.8 copy-done.2
  1.4 0.8 pack_first.1
  2.2 3.5 %collective-permute-start = (f32[9,4,128]{2,1,0:T(4,128)S(1)}, f32[9,4,128]{2,1,0:T(4,128)S(1)}, u32[]{:S(2)}, u32[]{:S(2)}) collective-permute-start(f32[9,4,128]{2,1,0:T(4,128)S(1)} %get-tuple-element.27), channel_id=1, source_target_pairs={{968,0},{984,16},{1000,32},{1016,48},{0,64},{16,80},{32,96},{48,11... | collective-permute-start | bytes 55304 | tf_op jit(solution)/shard_map/ppermute | solution.py:436
  5.8 16.8 %collective-permute-start.1 = (f32[9,4,128]{2,1,0:T(4,128)S(1)}, f32[9,4,128]{2,1,0:T(4,128)S(1)}, u32[]{:S(2)}, u32[]{:S(2)}) collective-permute-start(f32[9,4,128]{2,1,0:T(4,128)S(1)} %get-tuple-element.28), channel_id=1, source_target_pairs={{64,0},{80,16},{96,32},{112,48},{128,64},{144,80},{160,96},{176,11... | collective-permute-start | bytes 55304 | tf_op jit(solution)/shard_map/ppermute | solution.py:436
  22.6 0.0 collective-permute-done.low
  22.6 0.9 collective-permute-done.1.high
  23.4 14.9 %collective-permute-start.2 = (f32[36,4,128]{2,1,0:T(4,128)S(1)}, f32[36,4,128]{2,1,0:T(4,128)S(1)}, u32[]{:S(2)}, u32[]{:S(2)}) collective-permute-start(f32[36,4,128]{2,1,0:T(4,128)S(1)} %pack_swap.2), channel_id=1, source_target_pairs={{8,0},{0,8},{24,16},{16,24},{40,32},{32,40},{56,48},{48,56},{9,1},... | collective-permute-start | bytes 221192 | tf_op jit(solution)/shard_map/ppermute | solution.py:440
  38.3 9.6 %collective-permute-done.2.swapped = f32[36,4,128]{2,1,0:T(4,128)S(1)} collective-permute-done((f32[36,4,128]{2,1,0:T(4,128)S(1)}, f32[36,4,128]{2,1,0:T(4,128)S(1)}, u32[]{:S(2)}, u32[]{:S(2)}) %collective-permute-start.2) | collective-permute-done | bytes 73760 | tf_op jit(solution)/shard_map/ppermute | solution.py:440
  48.0 0.0 copy-start
  48.0 1.9 collective-permute-start.3
  49.9 2.7 %collective-permute-done.3.relayed = f32[15,4,128]{2,1,0:T(4,128)S(1)} collective-permute-done((f32[15,4,128]{2,1,0:T(4,128)S(1)}, f32[15,4,128]{2,1,0:T(4,128)S(1)}, u32[]{:S(2)}, u32[]{:S(2)}) %collective-permute-start.3) | collective-permute-done | bytes 30752 | tf_op jit(solution)/shard_map/ppermute | solution.py:447
  52.7 0.0 copy-start.1
  52.7 3.6 %collective-permute-start.4 = (f32[25,4,128]{2,1,0:T(4,128)S(1)}, f32[25,4,128]{2,1,0:T(4,128)S(1)}, u32[]{:S(2)}, u32[]{:S(2)}) collective-permute-start(f32[25,4,128]{2,1,0:T(4,128)S(1)} %get-tuple-element.30), channel_id=1, source_target_pairs={{7,0},{0,1},{1,2},{2,3},{3,4},{4,5},{5,6},{6,7},{15,8},{8,9},{9,10... | collective-permute-start | bytes 153608 | tf_op jit(solution)/shard_map/ppermute | solution.py:451
  56.3 0.0 collective-permute-start.5
  56.3 0.0 copy-done
  56.3 10.3 %own_pairs.2 = (f32[27,16,128]{2,1,0:T(8,128)S(1)}, f32[27,4,128]{2,1,0:T(4,128)S(1)}) custom-call(f32[27,4,128]{2,1,0:T(4,128)S(1)} %get-tuple-element.26.own, s32[3,3,3]{2,1,0:T(4,128)} %counts.5, s32[3,3,3,2,128]{4,3,2,1,0:T(2,128)S(1)} %bitcast.5), custom_call_target="tpu_custom_call" | custom-call | tf_op jit(solution)/shard_map/own_pairs/pallas_call | solution.py:26
  66.6 0.0 collective-permute-done.4.left
  66.7 0.0 collective-permute-done.5.right
  66.7 0.0 copy-done.1
  66.7 13.3 %step_one.1 = (f32[3,3,3,3,128]{4,3,2,1,0:T(4,128)S(1)}, f32[27,4,128]{2,1,0:T(4,128)S(1)}, f32[9,4,128]{2,1,0:T(4,128)S(1)}, f32[9,4,128]{2,1,0:T(4,128)S(1)}) custom-call(f32[75,4,128]{2,1,0:T(4,128)S(1)} %get-tuple-element.29.middle, f32[25,4,128]{2,1,0:T(4,128)S(1)} %collective-permute-done.4.left, f32[25,4,128]{2,1,0:T(4,128)S(1)} %collective-permute-done.5.right, ...), custom_call_target="tpu_custom_call" | custom-call | tf_op jit(solution)/shard_map/step_one/pallas_call | solution.py:26
  80.0 1.9 collective-permute-start.6
  81.9 6.2 %collective-permute-start.7 = (f32[9,4,128]{2,1,0:T(4,128)S(1)}, f32[9,4,128]{2,1,0:T(4,128)S(1)}, u32[]{:S(2)}, u32[]{:S(2)}) collective-permute-start(f32[9,4,128]{2,1,0:T(4,128)S(1)} %get-tuple-element.37), channel_id=1, source_target_pairs={{64,0},{80,16},{96,32},{112,48},{128,64},{144,80},{160,96},{176,11... | collective-permute-start | bytes 55304 | tf_op jit(solution)/shard_map/ppermute | solution.py:436
  88.1 0.0 collective-permute-done.6.low
  88.1 0.9 collective-permute-done.7.high
  89.0 20.8 %collective-permute-start.8 = (f32[36,4,128]{2,1,0:T(4,128)S(1)}, f32[36,4,128]{2,1,0:T(4,128)S(1)}, u32[]{:S(2)}, u32[]{:S(2)}) collective-permute-start(f32[36,4,128]{2,1,0:T(4,128)S(1)} %pack_swap.3), channel_id=1, source_target_pairs={{8,0},{0,8},{24,16},{16,24},{40,32},{32,40},{56,48},{48,56},{9,1},... | collective-permute-start | bytes 221192 | tf_op jit(solution)/shard_map/ppermute | solution.py:440
  109.7 2.8 %collective-permute-done.8.swapped = f32[36,4,128]{2,1,0:T(4,128)S(1)} collective-permute-done((f32[36,4,128]{2,1,0:T(4,128)S(1)}, f32[36,4,128]{2,1,0:T(4,128)S(1)}, u32[]{:S(2)}, u32[]{:S(2)}) %collective-permute-start.8) | collective-permute-done | bytes 73760 | tf_op jit(solution)/shard_map/ppermute | solution.py:440
  112.6 1.9 collective-permute-start.9
  114.5 2.7 %collective-permute-done.9.relayed = f32[15,4,128]{2,1,0:T(4,128)S(1)} collective-permute-done((f32[15,4,128]{2,1,0:T(4,128)S(1)}, f32[15,4,128]{2,1,0:T(4,128)S(1)}, u32[]{:S(2)}, u32[]{:S(2)}) %collective-permute-start.9) | collective-permute-done | bytes 30752 | tf_op jit(solution)/shard_map/ppermute | solution.py:447
  117.3 6.1 %collective-permute-start.10 = (f32[25,4,128]{2,1,0:T(4,128)S(1)}, f32[25,4,128]{2,1,0:T(4,128)S(1)}, u32[]{:S(2)}, u32[]{:S(2)}) collective-permute-start(f32[25,4,128]{2,1,0:T(4,128)S(1)} %get-tuple-element.39), channel_id=1, source_target_pairs={{7,0},{0,1},{1,2},{2,3},{3,4},{4,5},{5,6},{6,7},{15,8},{8,9},{9,10... | collective-permute-start | bytes 153608 | tf_op jit(solution)/shard_map/ppermute | solution.py:451
  123.4 0.0 collective-permute-start.11
  123.4 10.3 %own_pairs.3 = (f32[27,16,128]{2,1,0:T(8,128)S(1)}, f32[27,4,128]{2,1,0:T(4,128)S(1)}) custom-call(f32[27,4,128]{2,1,0:T(4,128)S(1)} %get-tuple-element.35.own, s32[3,3,3]{2,1,0:T(4,128)} %counts.5, s32[3,3,3,2,128]{4,3,2,1,0:T(2,128)S(1)} %bitcast.6), custom_call_target="tpu_custom_call" | custom-call | tf_op jit(solution)/shard_map/own_pairs/pallas_call | solution.py:26
  133.7 0.0 collective-permute-done.10.left
  133.7 0.0 collective-permute-done.11.right
  133.7 13.2 %step_two.1 = (f32[27,6,128]{2,1,0:T(8,128)S(1)}, f32[108,128]{1,0:T(8,128)S(1)}) custom-call(f32[75,4,128]{2,1,0:T(4,128)S(1)} %get-tuple-element.38.middle, f32[25,4,128]{2,1,0:T(4,128)S(1)} %collective-permute-done.10.left, f32[25,4,128]{2,1,0:T(4,128)S(1)} %collective-permute-done.11.right, f32[27,16,128]{2,1,0:T(8,128)S(1)} %get-tuple-element.41.acc_in, ...), custom_call_target="tpu_custom_call" | custom-call | tf_op jit(solution)/shard_map/step_two/pallas_call | solution.py:26
  147.0 13.1 %collective-permute-start.12 = (f32[108,128]{1,0:T(8,128)S(1)}, f32[108,128]{1,0:T(8,128)S(1)}, u32[]{:S(2)}, u32[]{:S(2)}) collective-permute-start(f32[108,128]{1,0:T(8,128)S(1)} %get-tuple-element.44), channel_id=1, source_target_pairs={{64,0},{80,16},{96,32},{112,48},{128,64},{144,80},{160,96},{176,11... | collective-permute-start | bytes 165896 | tf_op jit(solution)/shard_map/ppermute | solution.py:436
  160.1 1.2 collective-permute-done.12.high
  161.3 16.6 %collective-permute-start.13 = (f32[216,128]{1,0:T(8,128)S(1)}, f32[216,128]{1,0:T(8,128)S(1)}, u32[]{:S(2)}, u32[]{:S(2)}) collective-permute-start(f32[216,128]{1,0:T(8,128)S(1)} %pack_hand.1), channel_id=1, source_target_pairs={{8,0},{0,8},{24,16},{16,24},{40,32},{32,40},{56,48},{48,56},{9,1},... | collective-permute-start | bytes 331784 | tf_op jit(solution)/shard_map/ppermute | solution.py:440
  177.9 8.6 %collective-permute-done.13.swapped = f32[216,128]{1,0:T(8,128)S(1)} collective-permute-done((f32[216,128]{1,0:T(8,128)S(1)}, f32[216,128]{1,0:T(8,128)S(1)}, u32[]{:S(2)}, u32[]{:S(2)}) %collective-permute-start.13) | collective-permute-done | bytes 110624 | tf_op jit(solution)/shard_map/ppermute | solution.py:440
  186.5 0.7 collective-permute-start.14
  187.2 0.0 collective-permute-done.14.relayed
  187.2 0.1 pack_hand_side.1
  187.3 1.6 collective-permute-start.15
  188.8 0.6 copy.10
  189.5 20.3 %collective-permute-done.15.side = f32[300,128]{1,0:T(8,128)S(1)} collective-permute-done((f32[300,128]{1,0:T(8,128)S(1)}, f32[300,128]{1,0:T(8,128)S(1)}, u32[]{:S(2)}, u32[]{:S(2)}) %collective-permute-start.15) | collective-permute-done | bytes 153632 | tf_op jit(solution)/shard_map/ppermute | solution.py:451
  209.8 2.5 %place.1 = (f32[5,5,5,3,128]{4,3,2,1,0:T(4,128)}, f32[5,5,5,3,128]{4,3,2,1,0:T(4,128)}) custom-call(s32[16]{0:T(128)} %plan_z.1, s32[8,16]{1,0:T(8,128)} %bitcast.8, s32[8,8,16]{2,1,0:T(8,128)} %bitcast.7, f32[75,6,128]{2,1,0:T(8,128)S(1)} %get-tuple-element.45.middle, f32[300,128]{1,0:T(8,128)S(1)} %collective-permute-done.15.side), custom_call_target="tpu_custom_call" | custom-call | tf_op jit(solution)/shard_map/place/pallas_call | solution.py:26
  (8 shorter events, 0.2 us)
Async XLA Ops:
  0.6 0.8 copy-start.2
  2.2 20.3 %collective-permute-start = (f32[9,4,128]{2,1,0:T(4,128)S(1)}, f32[9,4,128]{2,1,0:T(4,128)S(1)}, u32[]{:S(2)}, u32[]{:S(2)}) collective-permute-start(f32[9,4,128]{2,1,0:T(4,128)S(1)} %get-tuple-element.27), channel_id=1, source_target_pairs={{968,0},{984,16},{1000,32},{1016,48},{0,64},{16,80},{32,96},{48,11... | collective-permute-start | bytes 55304 | tf_op jit(solution)/shard_map/ppermute | solution.py:436
  5.8 17.6 %collective-permute-start.1 = (f32[9,4,128]{2,1,0:T(4,128)S(1)}, f32[9,4,128]{2,1,0:T(4,128)S(1)}, u32[]{:S(2)}, u32[]{:S(2)}) collective-permute-start(f32[9,4,128]{2,1,0:T(4,128)S(1)} %get-tuple-element.28), channel_id=1, source_target_pairs={{64,0},{80,16},{96,32},{112,48},{128,64},{144,80},{160,96},{176,11... | collective-permute-start | bytes 55304 | tf_op jit(solution)/shard_map/ppermute | solution.py:436
  23.4 24.5 %collective-permute-start.2 = (f32[36,4,128]{2,1,0:T(4,128)S(1)}, f32[36,4,128]{2,1,0:T(4,128)S(1)}, u32[]{:S(2)}, u32[]{:S(2)}) collective-permute-start(f32[36,4,128]{2,1,0:T(4,128)S(1)} %pack_swap.2), channel_id=1, source_target_pairs={{8,0},{0,8},{24,16},{16,24},{40,32},{32,40},{56,48},{48,56},{9,1},... | collective-permute-start | bytes 221192 | tf_op jit(solution)/shard_map/ppermute | solution.py:440
  48.0 8.4 %copy-start = (s32[2,3,3,3,128]{4,0,3,2,1:T(2,128)S(1)}, s32[2,3,3,3,128]{4,0,3,2,1:T(2,128)}, u32[]{:S(2)}) copy-start(s32[2,3,3,3,128]{4,0,3,2,1:T(2,128)} %param.10) | copy-start | bytes 82948
  48.0 4.6 %collective-permute-start.3 = (f32[15,4,128]{2,1,0:T(4,128)S(1)}, f32[15,4,128]{2,1,0:T(4,128)S(1)}, u32[]{:S(2)}, u32[]{:S(2)}) collective-permute-start(f32[15,4,128]{2,1,0:T(4,128)S(1)} %pack_relay.2), channel_id=1, source_target_pairs={{48,0},{24,8},{0,16},{40,24},{16,32},{56,40},{32,48},{8,56},{49,1}... | collective-permute-start | bytes 92168 | tf_op jit(solution)/shard_map/ppermute | solution.py:447
  52.7 14.0 %copy-start.1 = (f32[3,3,3,3,128]{4,3,2,1,0:T(4,128)S(1)}, f32[3,3,3,3,128]{4,3,2,1,0:T(4,128)}, u32[]{:S(2)}) copy-start(f32[3,3,3,3,128]{4,3,2,1,0:T(4,128)} %vel.1) | copy-start | bytes 124420
  52.7 14.0 %collective-permute-start.4 = (f32[25,4,128]{2,1,0:T(4,128)S(1)}, f32[25,4,128]{2,1,0:T(4,128)S(1)}, u32[]{:S(2)}, u32[]{:S(2)}) collective-permute-start(f32[25,4,128]{2,1,0:T(4,128)S(1)} %get-tuple-element.30), channel_id=1, source_target_pairs={{7,0},{0,1},{1,2},{2,3},{3,4},{4,5},{5,6},{6,7},{15,8},{8,9},{9,10... | collective-permute-start | bytes 153608 | tf_op jit(solution)/shard_map/ppermute | solution.py:451
  56.3 10.4 %collective-permute-start.5 = (f32[25,4,128]{2,1,0:T(4,128)S(1)}, f32[25,4,128]{2,1,0:T(4,128)S(1)}, u32[]{:S(2)}, u32[]{:S(2)}) collective-permute-start(f32[25,4,128]{2,1,0:T(4,128)S(1)} %get-tuple-element.31), channel_id=1, source_target_pairs={{1,0},{2,1},{3,2},{4,3},{5,4},{6,5},{7,6},{0,7},{9,8},{10,9},{11,1... | collective-permute-start | bytes 153608 | tf_op jit(solution)/shard_map/ppermute | solution.py:451
  80.0 8.1 %collective-permute-start.6 = (f32[9,4,128]{2,1,0:T(4,128)S(1)}, f32[9,4,128]{2,1,0:T(4,128)S(1)}, u32[]{:S(2)}, u32[]{:S(2)}) collective-permute-start(f32[9,4,128]{2,1,0:T(4,128)S(1)} %get-tuple-element.36), channel_id=1, source_target_pairs={{968,0},{984,16},{1000,32},{1016,48},{0,64},{16,80},{32,96},{48,11... | collective-permute-start | bytes 55304 | tf_op jit(solution)/shard_map/ppermute | solution.py:436
  81.9 7.1 %collective-permute-start.7 = (f32[9,4,128]{2,1,0:T(4,128)S(1)}, f32[9,4,128]{2,1,0:T(4,128)S(1)}, u32[]{:S(2)}, u32[]{:S(2)}) collective-permute-start(f32[9,4,128]{2,1,0:T(4,128)S(1)} %get-tuple-element.37), channel_id=1, source_target_pairs={{64,0},{80,16},{96,32},{112,48},{128,64},{144,80},{160,96},{176,11... | collective-permute-start | bytes 55304 | tf_op jit(solution)/shard_map/ppermute | solution.py:436
  89.0 23.6 %collective-permute-start.8 = (f32[36,4,128]{2,1,0:T(4,128)S(1)}, f32[36,4,128]{2,1,0:T(4,128)S(1)}, u32[]{:S(2)}, u32[]{:S(2)}) collective-permute-start(f32[36,4,128]{2,1,0:T(4,128)S(1)} %pack_swap.3), channel_id=1, source_target_pairs={{8,0},{0,8},{24,16},{16,24},{40,32},{32,40},{56,48},{48,56},{9,1},... | collective-permute-start | bytes 221192 | tf_op jit(solution)/shard_map/ppermute | solution.py:440
  112.6 4.6 %collective-permute-start.9 = (f32[15,4,128]{2,1,0:T(4,128)S(1)}, f32[15,4,128]{2,1,0:T(4,128)S(1)}, u32[]{:S(2)}, u32[]{:S(2)}) collective-permute-start(f32[15,4,128]{2,1,0:T(4,128)S(1)} %pack_relay.3), channel_id=1, source_target_pairs={{48,0},{24,8},{0,16},{40,24},{16,32},{56,40},{32,48},{8,56},{49,1}... | collective-permute-start | bytes 92168 | tf_op jit(solution)/shard_map/ppermute | solution.py:447
  117.3 16.5 %collective-permute-start.10 = (f32[25,4,128]{2,1,0:T(4,128)S(1)}, f32[25,4,128]{2,1,0:T(4,128)S(1)}, u32[]{:S(2)}, u32[]{:S(2)}) collective-permute-start(f32[25,4,128]{2,1,0:T(4,128)S(1)} %get-tuple-element.39), channel_id=1, source_target_pairs={{7,0},{0,1},{1,2},{2,3},{3,4},{4,5},{5,6},{6,7},{15,8},{8,9},{9,10... | collective-permute-start | bytes 153608 | tf_op jit(solution)/shard_map/ppermute | solution.py:451
  123.4 10.4 %collective-permute-start.11 = (f32[25,4,128]{2,1,0:T(4,128)S(1)}, f32[25,4,128]{2,1,0:T(4,128)S(1)}, u32[]{:S(2)}, u32[]{:S(2)}) collective-permute-start(f32[25,4,128]{2,1,0:T(4,128)S(1)} %get-tuple-element.40), channel_id=1, source_target_pairs={{1,0},{2,1},{3,2},{4,3},{5,4},{6,5},{7,6},{0,7},{9,8},{10,9},{11,1... | collective-permute-start | bytes 153608 | tf_op jit(solution)/shard_map/ppermute | solution.py:451
  147.0 14.3 %collective-permute-start.12 = (f32[108,128]{1,0:T(8,128)S(1)}, f32[108,128]{1,0:T(8,128)S(1)}, u32[]{:S(2)}, u32[]{:S(2)}) collective-permute-start(f32[108,128]{1,0:T(8,128)S(1)} %get-tuple-element.44), channel_id=1, source_target_pairs={{64,0},{80,16},{96,32},{112,48},{128,64},{144,80},{160,96},{176,11... | collective-permute-start | bytes 165896 | tf_op jit(solution)/shard_map/ppermute | solution.py:436
  161.3 25.2 %collective-permute-start.13 = (f32[216,128]{1,0:T(8,128)S(1)}, f32[216,128]{1,0:T(8,128)S(1)}, u32[]{:S(2)}, u32[]{:S(2)}) collective-permute-start(f32[216,128]{1,0:T(8,128)S(1)} %pack_hand.1), channel_id=1, source_target_pairs={{8,0},{0,8},{24,16},{16,24},{40,32},{32,40},{56,48},{48,56},{9,1},... | collective-permute-start | bytes 331784 | tf_op jit(solution)/shard_map/ppermute | solution.py:440
  186.5 0.7 collective-permute-start.14
  187.3 22.5 %collective-permute-start.15 = (f32[300,128]{1,0:T(8,128)S(1)}, f32[300,128]{1,0:T(8,128)S(1)}, u32[]{:S(2)}, u32[]{:S(2)}) collective-permute-start(f32[300,128]{1,0:T(8,128)S(1)} %get-tuple-element.46), channel_id=1, source_target_pairs={{1,0},{2,1},{3,2},{4,3},{5,4},{6,5},{7,6},{0,7},{9,8},{10,9},{11,1... | collective-permute-start | bytes 460808 | tf_op jit(solution)/shard_map/ppermute | solution.py:451

commit v2 on v1

--- a/solution.py
+++ b/solution.py
@@ -27,7 +27,9 @@
         kernel,
         name=name,
         out_shape=[
-            (jax.ShapeDtypeStruct if to_hbm else pltpu.VMEM)(shape, F32) for shape in outs
+            jax.ShapeDtypeStruct(shape, F32) if to_hbm
+            else pltpu.VMEM(shape, F32) if isinstance(shape, tuple) else shape
+            for shape in outs
         ],
         in_specs=specs,
         out_specs=[V] * len(outs),
@@ -173,7 +175,8 @@
     x_ref[at] = rows[16:32].astype(BF16)
 
 
-AHEAD = 8
+AHEAD = 12
+OWN_CUTS = (2, 5)
 
 
 def push_rows(acc_ref, blocks, b_ref, x_ref, a_ref):
@@ -217,21 +220,16 @@
     return z, step - 2 * z
 
 
-def own_pairs(own, counts, bonds, acc_out, bond_out, b_ref, x_ref, a_ref):
-    def prepare(row, _):
-        z, y = row // 3, row % 3
-        for x in range(3):
-            coords, alive = scaled_cell(own[3 * row + x], z, y, x)
-            store_operands(partner_rows(coords, alive), 3 * row + x, b_ref, x_ref)
-            a_ref[row, :, N * x : N * (x + 1)] = own_rows(coords).astype(BF16)
-            acc_out[3 * row + x] = jnp.zeros((16, N), F32)
-            bond_out[3 * row + x] = bond_cell(
-                own[3 * row + x], bonds[z, y, x, 0:1], bonds[z, y, x, 1:2], counts[z, y, x],
-            )
-        return 0
-
-    lax.fori_loop(0, 9, prepare, 0)
-
+def each(count, group, body):
+    def several(start, _):
+        for step in range(group):
+            body(group * start + step, 0)
+        return 0
+
+    lax.fori_loop(0, count // group, several, 0)
+
+
+def own_sweeps(first, last, acc, b_ref, x_ref, a_ref):
     def sweep(step, _):
         z, other = z_pair(step)
         blocks = [
@@ -240,10 +238,32 @@
             for near in range(max(0, y - 1), min(2, y + 1) + 1)
             for x in range(3)
         ]
-        push_rows(acc_out, blocks, b_ref, x_ref, a_ref)
-        return 0
-
-    lax.fori_loop(0, 7, sweep, 0)
+        push_rows(acc, blocks, b_ref, x_ref, a_ref)
+        return 0
+
+    lax.fori_loop(first, last, sweep, 0)
+
+
+def own_start(own, counts, bonds, acc, bond_out, b_ref, x_ref, a_ref):
+    def prepare(row, _):
+        z, y = row // 3, row % 3
+        for x in range(3):
+            coords, alive = scaled_cell(own[3 * row + x], z, y, x)
+            store_operands(partner_rows(coords, alive), 3 * row + x, b_ref, x_ref)
+            a_ref[row, :, N * x : N * (x + 1)] = own_rows(coords).astype(BF16)
+            acc[3 * row + x] = jnp.zeros((16, N), F32)
+            bond_out[3 * row + x] = bond_cell(
+                own[3 * row + x], bonds[z, y, x, 0:1], bonds[z, y, x, 1:2], counts[z, y, x]
+            )
+        return 0
+
+    each(9, 3, prepare)
+    own_sweeps(0, OWN_CUTS[0], acc, b_ref, x_ref, a_ref)
+
+
+def own_more(acc_in, b_ref, x_ref, a_ref, acc, *, first, last):
+    acc[...] = acc_in[...]
+    own_sweeps(first, last, acc, b_ref, x_ref, a_ref)
 
 
 def bond_cell(cell, heads, tails, count):
@@ -260,27 +280,29 @@
     return -(back[0:4] + back[4:8] + back[8:12])
 
 
-def other_pairs(middle, left, right, acc_in, acc, b_ref, x_ref, a_ref):
-    def prepare(row, _):
-        p, y = row // 5 - 1, row % 5 - 1
-        for x in range(-1, 4):
-            cell = left[row] if x == -1 else right[row] if x == 3 else middle[3 * row + x]
-            coords, alive = scaled_cell(cell, p, y, x)
-            store_operands(partner_rows(coords, alive), 5 * row + x + 1, b_ref, x_ref)
-        return 0
-
-    lax.fori_loop(0, 25, prepare, 0)
-
-    def prepare_own(row, _):
-        z, y = row // 3, row % 3
+def other_pairs(middle, left, right, acc_in, a_ref, acc, b_ref, x_ref):
+    acc[...] = acc_in[...]
+
+    def prepare(cell, row, x):
+        coords, alive = scaled_cell(cell, row // 5 - 1, row % 5 - 1, x)
+        store_operands(partner_rows(coords, alive), 5 * row + x + 1, b_ref, x_ref)
+
+    def prepare_sides(row, _):
+        prepare(left[row], row, -1)
+        prepare(right[row], row, 3)
+        return 0
+
+    each(25, 5, prepare_sides)
+
+    def prepare_around(step, _):
+        inner = step - 10
+        row = jnp.where(step < 5, step, jnp.where(step < 10, step + 15, 0))
+        row = jnp.where(step < 10, row, 5 * (1 + inner // 2) + 4 * (inner % 2))
         for x in range(3):
-            cell = middle[3 * (5 * (z + 1) + y + 1) + x]
-            coords, alive = scaled_cell(cell, z, y, x)
-            a_ref[row, :, N * x : N * (x + 1)] = own_rows(coords).astype(BF16)
-            acc[3 * row + x] = acc_in[3 * row + x]
-        return 0
-
-    lax.fori_loop(0, 9, prepare_own, 0)
+            prepare(middle[3 * row + x], row, x)
+        return 0
+
+    each(16, 4, prepare_around)
 
     def row_blocks(row, at_row, columns, tag):
         return [(row, x, 5 * at_row + x + 1, tag) for x in columns]
@@ -309,9 +331,9 @@
 
 
 def step_one(
-    middle, left, right, acc_in, bond, vel, forces, own, top, bottom, acc, b_ref, x_ref, a_ref
+    middle, left, right, acc_in, bond, a_ref, vel, forces, own, top, bottom, acc, b_ref, x_ref
 ):
-    other_pairs(middle, left, right, acc_in, acc, b_ref, x_ref, a_ref)
+    other_pairs(middle, left, right, acc_in, a_ref, acc, b_ref, x_ref)
     for z in range(3):
         for y in range(3):
             for x in range(3):
@@ -331,8 +353,8 @@
                     forces[k, z, y, x : x + 1, :] = force[k : k + 1]
 
 
-def step_two(middle, left, right, acc_in, bond, carried, bottom, acc, b_ref, x_ref, a_ref):
-    other_pairs(middle, left, right, acc_in, acc, b_ref, x_ref, a_ref)
+def step_two(middle, left, right, acc_in, bond, a_ref, carried, message, acc, b_ref, x_ref):
+    other_pairs(middle, left, right, acc_in, a_ref, acc, b_ref, x_ref)
     for z in range(3):
         for y in range(3):
             for x in range(3):
@@ -342,12 +364,13 @@
                 force = (cell_force(acc[at], coords) + bond[at][0:3]) * cell[3:4]
                 both = jnp.concatenate([cell[0:3] * cell[3:4], force], axis=0)
                 carried[at] = both
-                if z < 2:
-                    bottom[6 * at : 6 * at + 6] = both
+                if (z, y, x) in HAND_AT:
+                    to = HAND_AT[z, y, x]
+                    message[6 * to : 6 * to + 6] = both
 
 
 HAND_CELLS = [
-    (p, y, x) for p in range(5) for y in range(2 if p < 3 else 3) for x in range(3)
+    (p, y, x) for p in range(3) for y in range(3 if p < 2 else 2) for x in range(3)
 ]
 HAND_AT = {cell: at for at, cell in enumerate(HAND_CELLS)}
 
@@ -356,42 +379,48 @@
     return ref[6 * at : 6 * at + 6]
 
 
-def pack_hand(own, high, out):
-    for (p, y, x), at in HAND_AT.items():
-        value = own[9 * p + 3 * y + x] if p < 3 else rows6(high, 9 * (p - 3) + 3 * y + x)
-        out[6 * at : 6 * at + 6] = value
-
-
-def partner_six(high, swapped, p, y, x):
-    there = rows6(swapped, HAND_AT[p, y, x])
-    if p < 3:
-        return there
-    return jnp.where(highest_plane(), rows6(high, 9 * (p - 3) + 3 * y + x), there)
-
-
-def pack_hand_relay(high, swapped, out):
+def pack_up(own, swapped, out):
+    for p in range(2):
+        for y in range(3):
+            for x in range(3):
+                at = 9 * p + 3 * y + x
+                out[6 * at : 6 * at + 6] = own[at]
+                out[6 * (18 + at) : 6 * (18 + at) + 6] = rows6(swapped, HAND_AT[p, y, x])
+
+
+def above(upper, p, y, x, partner):
+    at = 9 * (p - 3) + 3 * y + x
+    same, crossed = rows6(upper, at), rows6(upper, 18 + at)
+    if partner:
+        same, crossed = crossed, same
+    return jnp.where(highest_plane(), crossed, same)
+
+
+def partner_six(swapped, upper, p, y, x):
+    return rows6(swapped, HAND_AT[p, y, x]) if p < 3 else above(upper, p, y, x, True)
+
+
+def pack_hand_relay(swapped, upper, out):
     for p in range(5):
         for y in range(2):
             for x in range(3):
                 at = 6 * p + 3 * y + x
-                out[6 * at : 6 * at + 6] = partner_six(high, swapped, p, y, x)
-
-
-def pack_hand_side(own, high, swapped, relayed, middle, side):
+                out[6 * at : 6 * at + 6] = partner_six(swapped, upper, p, y, x)
+
+
+def pack_hand_side(own, swapped, upper, relayed, middle, side):
     even = even_column()
     for p in range(5):
         for y in range(5):
             for x in range(3):
                 if y >= 3:
-                    near = partner_six(high, swapped, p, y - 3, x)
+                    near = partner_six(swapped, upper, p, y - 3, x)
                     far = rows6(relayed, 6 * p + 3 * (y - 3) + x)
                     value = jnp.where(even, near, far)
                 elif p < 3:
                     value = own[9 * p + 3 * y + x]
                 else:
-                    near = rows6(high, 9 * (p - 3) + 3 * y + x)
-                    far = rows6(swapped, HAND_AT[p, y, x])
-                    value = jnp.where(highest_plane(), far, near)
+                    value = above(upper, p, y, x, False)
                 middle[15 * p + 3 * y + x] = value
                 if x < 2:
                     at = 10 * p + 2 * y + x
@@ -456,26 +485,37 @@
     high = z_ring(bottom, -1)
     (message,) = call(pack_swap, "pack_swap", (own, low, high), [(36, 4, N)])
     swapped = swap(message)
-    acc, bond = call(
-        own_pairs, "own_pairs", (own, counts, bonds), [(27, 16, N), (27, 4, N)],
-        [pltpu.VMEM((27, N, 32), BF16), pltpu.VMEM((27, 16, N), BF16),
-         pltpu.VMEM((9, 32, 3 * N), BF16)],
-        [V, S, V],
+    acc, bond, *operands = call(
+        own_start, "own_start", (own, counts, bonds),
+        [(27, 16, N), (27, 4, N), pltpu.VMEM((27, N, 32), BF16),
+         pltpu.VMEM((27, 16, N), BF16), pltpu.VMEM((9, 32, 3 * N), BF16)],
+        (), [V, S, V],
     )
     (message,) = call(
-        pack_relay, "pack_relay", (low, high, swapped), [(15, 4, N)]
+        after(pack_relay), "pack_relay", (acc, low, high, swapped), [(15, 4, N)]
     )
     relayed = relay(message)
-    middle, left, right = call(
-        pack_middle, "pack_middle", (own, low, high, swapped, relayed),
-        [(75, 4, N), (25, 4, N), (25, 4, N)],
-    )
-    return middle, along_x(right, 1), along_x(left, -1), acc, bond
+    for part in range(2):
+        if part == 1:
+            middle, left, right = call(
+                after(pack_middle), "pack_middle", (acc, own, low, high, swapped, relayed),
+                [(75, 4, N), (25, 4, N), (25, 4, N)],
+            )
+        cuts = OWN_CUTS + (7,)
+        (acc,) = call(
+            functools.partial(own_more, first=cuts[part], last=cuts[part + 1]),
+            f"own_more_{part}", (acc, *operands), [(27, 16, N)],
+        )
+    return middle, along_x(right, 1), along_x(left, -1), acc, bond, operands[2]
+
+
+def after(kernel):
+    return lambda waited, *refs: kernel(*refs)
 
 
 PAIR_SCRATCH = [
     pltpu.VMEM((27, 16, N), F32), pltpu.VMEM((125, N, 32), BF16),
-    pltpu.VMEM((125, 16, N), BF16), pltpu.VMEM((9, 32, 3 * N), BF16),
+    pltpu.VMEM((125, 16, N), BF16),
 ]
 
 
@@ -485,25 +525,20 @@
         pack_first, "pack_first", (positions, counts), [(27, 4, N), (9, 4, N), (9, 4, N)], (),
         [V, S],
     )
-    middle, left, right, acc, bond = halo_and_own(own, top, bottom, counts, bonds)
+    halo = halo_and_own(own, top, bottom, counts, bonds)
     forces_first, own, top, bottom = call(
-        step_one, "step_one", (middle, left, right, acc, bond, velocities),
+        step_one, "step_one", (*halo, velocities),
         [(3, 3, 3, 3, N), (27, 4, N), (9, 4, N), (9, 4, N)], PAIR_SCRATCH,
     )
-    middle, left, right, acc, bond = halo_and_own(own, top, bottom, counts, bonds)
-    own, bottom = call(
-        step_two, "step_two", (middle, left, right, acc, bond), [(27, 6, N), (108, N)],
-        PAIR_SCRATCH,
-    )
-    high = z_ring(bottom, -1)
-    (message,) = call(pack_hand, "pack_hand", (own, high), [(216, N)])
+    halo = halo_and_own(own, top, bottom, counts, bonds)
+    own, message = call(step_two, "step_two", halo, [(27, 6, N), (144, N)], PAIR_SCRATCH)
     swapped = swap(message)
-    (message,) = call(
-        pack_hand_relay, "pack_hand_relay", (high, swapped), [(180, N)]
-    )
+    (message,) = call(pack_up, "pack_up", (own, swapped), [(216, N)])
+    upper = z_ring(message, -1)
+    (message,) = call(pack_hand_relay, "pack_hand_relay", (swapped, upper), [(180, N)])
     relayed = relay(message, True)
     middle, side = call(
-        pack_hand_side, "pack_hand_side", (own, high, swapped, relayed),
+        pack_hand_side, "pack_hand_side", (own, swapped, upper, relayed),
         [(75, 6, N), (300, N)],
     )
     side = along_x(side, -1)

time: 213 us -> 183 us (0.86)
  the two profiles are of different devices: /device:TPU:31 before, /device:TPU:7 now
where the time goes in v2:
time: 183 us; the launch traced here: 182 us
  starting transfers between devices  115 us (63%)
  Pallas kernels  42.8 us (23%)
  waiting for transfers between devices  22.3 us (12%)
    ppermute x3, starting transfers between devices, swap(): return lax.ppermute(block, 'gy', [(i ^ 1, i) for i in range(8)])  55.5 us
    ppermute x5, starting transfers between devices, z_ring(): return lax.ppermute(block, ('gz', 'gy'), route)  45.5 us
    pallas_call x19, Pallas kernels, call(): pl.pallas_call(kernel, name=name, out_shape=[jax.ShapeDtypeStruct(shape,...  42.8 us
    ppermute x5, waiting for transfers between devices, along_x(): lax.ppermute(block, 'gx', [((i - distance) % 8, i) for i in range(8)])  9.68 us
    ppermute x3, waiting for transfers between devices, swap(): return lax.ppermute(block, 'gy', [(i ^ 1, i) for i in range(8)])  7.88 us
    ppermute x5, starting transfers between devices, along_x(): lax.ppermute(block, 'gx', [((i - distance) % 8, i) for i in range(8)])  7.71 us
    ppermute x3, starting transfers between devices, relay(): return lax.ppermute(block, 'gy', pairs)  5.79 us
  transfers between devices with their start and end apart: 16, of which 9 were waited for; matrix products, arithmetic and copies ran while one was open for 0% of the time, Pallas kernels for 10%

profile of v2, /device:TPU:7, one launch (start us, length us, event | category | flops | bytes accessed | tf_op | source)
XLA Modules:
  0.0 182.0 jit_solution(17654307412914550455)
XLA Ops:
  0.6 0.0 copy-start.2
  0.6 0.8 copy-done.2
  1.4 0.8 pack_first.1
  2.2 3.5 %collective-permute-start = (f32[9,4,128]{2,1,0:T(4,128)S(1)}, f32[9,4,128]{2,1,0:T(4,128)S(1)}, u32[]{:S(2)}, u32[]{:S(2)}) collective-permute-start(f32[9,4,128]{2,1,0:T(4,128)S(1)} %get-tuple-element.37), channel_id=1, source_target_pairs={{968,0},{984,16},{1000,32},{1016,48},{0,64},{16,80},{32,96},{48,11... | collective-permute-start | bytes 55304 | tf_op jit(solution)/shard_map/ppermute | solution.py:465
  5.8 16.8 %collective-permute-start.1 = (f32[9,4,128]{2,1,0:T(4,128)S(1)}, f32[9,4,128]{2,1,0:T(4,128)S(1)}, u32[]{:S(2)}, u32[]{:S(2)}) collective-permute-start(f32[9,4,128]{2,1,0:T(4,128)S(1)} %get-tuple-element.38), channel_id=1, source_target_pairs={{64,0},{80,16},{96,32},{112,48},{128,64},{144,80},{160,96},{176,11... | collective-permute-start | bytes 55304 | tf_op jit(solution)/shard_map/ppermute | solution.py:465
  22.6 0.0 collective-permute-done.low.refs_0_.refs_1_
  22.6 0.9 collective-permute-done.1.high.refs_1_.refs_2_
  23.4 0.0 copy-start
  23.5 14.9 %collective-permute-start.2 = (f32[36,4,128]{2,1,0:T(4,128)S(1)}, f32[36,4,128]{2,1,0:T(4,128)S(1)}, u32[]{:S(2)}, u32[]{:S(2)}) collective-permute-start(f32[36,4,128]{2,1,0:T(4,128)S(1)} %pack_swap.2), channel_id=1, source_target_pairs={{8,0},{0,8},{24,16},{16,24},{40,32},{32,40},{56,48},{48,56},{9,1},... | collective-permute-start | bytes 221192 | tf_op jit(solution)/shard_map/ppermute | solution.py:469
  38.3 0.0 copy-done
  38.3 5.0 %own_start.2 = (f32[27,16,128]{2,1,0:T(8,128)S(1)}, f32[27,4,128]{2,1,0:T(4,128)S(1)}, bf16[27,128,32]{2,1,0:T(8,128)(2,1)S(1)}, bf16[27,16,128]{2,1,0:T(8,128)(2,1)S(1)}, bf16[9,32,384]{2,1,0:T(8,128)(2,1)S(1)}) custom-call(f32[27,4,128]{2,1,0:T(4,128)S(1)} %get-tuple-element.32.own.refs_0_, s32[3,3,3]{2,1,0:T(4,128)} %counts.5, ...), custom_call_target="tpu_custom_call" | custom-call | tf_op jit(solution)/shard_map/own_start/pallas_call | solution.py:26
  43.4 4.6 %collective-permute-done.2.refs_2_.refs_3_ = f32[36,4,128]{2,1,0:T(4,128)S(1)} collective-permute-done((f32[36,4,128]{2,1,0:T(4,128)S(1)}, f32[36,4,128]{2,1,0:T(4,128)S(1)}, u32[]{:S(2)}, u32[]{:S(2)}) %collective-permute-start.2) | collective-permute-done | bytes 73760 | tf_op jit(solution)/shard_map/ppermute | solution.py:469
  48.0 3.2 %collective-permute-start.3 = (f32[15,4,128]{2,1,0:T(4,128)S(1)}, f32[15,4,128]{2,1,0:T(4,128)S(1)}, u32[]{:S(2)}, u32[]{:S(2)}) collective-permute-start(f32[15,4,128]{2,1,0:T(4,128)S(1)} %pack_relay.2), channel_id=1, source_target_pairs={{48,0},{24,8},{0,16},{40,24},{16,32},{56,40},{32,48},{8,56},{49,1}... | collective-permute-start | bytes 92168 | tf_op jit(solution)/shard_map/ppermute | solution.py:476
  51.2 2.7 %own_more_0.2.waited.acc_in = f32[27,16,128]{2,1,0:T(8,128)S(1)} custom-call(f32[27,16,128]{2,1,0:T(8,128)S(1)} %get-tuple-element.33.acc_in.waited, bf16[27,128,32]{2,1,0:T(8,128)(2,1)S(1)} %get-tuple-element.34.b_ref, bf16[27,16,128]{2,1,0:T(8,128)(2,1)S(1)} %get-tuple-element.35.x_ref, bf16[9,32,384]{2,1,0:T(8,128)(2,1)S(1)} %get-tuple-element.36.a_ref), custom_call_target="tpu_custom_call" | custom-call | tf_op jit(solution)/shard_map/own_more_0/pallas_call | solution.py:26
  53.9 0.0 collective-permute-done.3.refs_4_
  53.9 3.6 %collective-permute-start.4 = (f32[25,4,128]{2,1,0:T(4,128)S(1)}, f32[25,4,128]{2,1,0:T(4,128)S(1)}, u32[]{:S(2)}, u32[]{:S(2)}) collective-permute-start(f32[25,4,128]{2,1,0:T(4,128)S(1)} %get-tuple-element.40), channel_id=1, source_target_pairs={{7,0},{0,1},{1,2},{2,3},{3,4},{4,5},{5,6},{6,7},{15,8},{8,9},{9,10... | collective-permute-start | bytes 153608 | tf_op jit(solution)/shard_map/ppermute | solution.py:480
  57.5 0.0 copy-start.1
  57.5 0.0 collective-permute-start.5
  57.5 1.8 own_more_1.2.acc_in
  59.3 0.0 collective-permute-done.4.left
  59.3 3.0 %collective-permute-done.5.right = f32[25,4,128]{2,1,0:T(4,128)S(1)} collective-permute-done((f32[25,4,128]{2,1,0:T(4,128)S(1)}, f32[25,4,128]{2,1,0:T(4,128)S(1)}, u32[]{:S(2)}, u32[]{:S(2)}) %collective-permute-start.5) | collective-permute-done | bytes 51232 | tf_op jit(solution)/shard_map/ppermute | solution.py:480
  62.3 0.0 copy-done.1
  62.3 10.2 %step_one.1 = (f32[3,3,3,3,128]{4,3,2,1,0:T(4,128)S(1)}, f32[27,4,128]{2,1,0:T(4,128)S(1)}, f32[9,4,128]{2,1,0:T(4,128)S(1)}, f32[9,4,128]{2,1,0:T(4,128)S(1)}) custom-call(f32[75,4,128]{2,1,0:T(4,128)S(1)} %get-tuple-element.39.middle, f32[25,4,128]{2,1,0:T(4,128)S(1)} %collective-permute-done.4.left, f32[25,4,128]{2,1,0:T(4,128)S(1)} %collective-permute-done.5.right, ...), custom_call_target="tpu_custom_call" | custom-call | tf_op jit(solution)/shard_map/step_one/pallas_call | solution.py:26
  72.5 1.9 %collective-permute-start.6 = (f32[9,4,128]{2,1,0:T(4,128)S(1)}, f32[9,4,128]{2,1,0:T(4,128)S(1)}, u32[]{:S(2)}, u32[]{:S(2)}) collective-permute-start(f32[9,4,128]{2,1,0:T(4,128)S(1)} %get-tuple-element.49), channel_id=1, source_target_pairs={{968,0},{984,16},{1000,32},{1016,48},{0,64},{16,80},{32,96},{48,11... | collective-permute-start | bytes 55304 | tf_op jit(solution)/shard_map/ppermute | solution.py:465
  74.4 5.6 %collective-permute-start.7 = (f32[9,4,128]{2,1,0:T(4,128)S(1)}, f32[9,4,128]{2,1,0:T(4,128)S(1)}, u32[]{:S(2)}, u32[]{:S(2)}) collective-permute-start(f32[9,4,128]{2,1,0:T(4,128)S(1)} %get-tuple-element.50), channel_id=1, source_target_pairs={{64,0},{80,16},{96,32},{112,48},{128,64},{144,80},{160,96},{176,11... | collective-permute-start | bytes 55304 | tf_op jit(solution)/shard_map/ppermute | solution.py:465
  80.0 0.0 collective-permute-done.6.low.refs_0_.refs_1_
  80.0 0.9 collective-permute-done.7.high.refs_1_.refs_2_
  80.9 20.5 %collective-permute-start.8 = (f32[36,4,128]{2,1,0:T(4,128)S(1)}, f32[36,4,128]{2,1,0:T(4,128)S(1)}, u32[]{:S(2)}, u32[]{:S(2)}) collective-permute-start(f32[36,4,128]{2,1,0:T(4,128)S(1)} %pack_swap.3), channel_id=1, source_target_pairs={{8,0},{0,8},{24,16},{16,24},{40,32},{32,40},{56,48},{48,56},{9,1},... | collective-permute-start | bytes 221192 | tf_op jit(solution)/shard_map/ppermute | solution.py:469
  101.4 5.0 %own_start.3 = (f32[27,16,128]{2,1,0:T(8,128)S(1)}, f32[27,4,128]{2,1,0:T(4,128)S(1)}, bf16[27,128,32]{2,1,0:T(8,128)(2,1)S(1)}, bf16[27,16,128]{2,1,0:T(8,128)(2,1)S(1)}, bf16[9,32,384]{2,1,0:T(8,128)(2,1)S(1)}) custom-call(f32[27,4,128]{2,1,0:T(4,128)S(1)} %get-tuple-element.44.own.refs_0_, s32[3,3,3]{2,1,0:T(4,128)} %counts.5, ...), custom_call_target="tpu_custom_call" | custom-call | tf_op jit(solution)/shard_map/own_start/pallas_call | solution.py:26
  106.4 0.0 collective-permute-done.8.refs_2_.refs_3_
  106.5 1.9 %collective-permute-start.9 = (f32[15,4,128]{2,1,0:T(4,128)S(1)}, f32[15,4,128]{2,1,0:T(4,128)S(1)}, u32[]{:S(2)}, u32[]{:S(2)}) collective-permute-start(f32[15,4,128]{2,1,0:T(4,128)S(1)} %pack_relay.3), channel_id=1, source_target_pairs={{48,0},{24,8},{0,16},{40,24},{16,32},{56,40},{32,48},{8,56},{49,1}... | collective-permute-start | bytes 92168 | tf_op jit(solution)/shard_map/ppermute | solution.py:476
  108.4 2.6 %own_more_0.3.waited.acc_in = f32[27,16,128]{2,1,0:T(8,128)S(1)} custom-call(f32[27,16,128]{2,1,0:T(8,128)S(1)} %get-tuple-element.45.acc_in.waited, bf16[27,128,32]{2,1,0:T(8,128)(2,1)S(1)} %get-tuple-element.46.b_ref, bf16[27,16,128]{2,1,0:T(8,128)(2,1)S(1)} %get-tuple-element.47.x_ref, bf16[9,32,384]{2,1,0:T(8,128)(2,1)S(1)} %get-tuple-element.48.a_ref), custom_call_target="tpu_custom_call" | custom-call | tf_op jit(solution)/shard_map/own_more_0/pallas_call | solution.py:26
  111.1 1.3 collective-permute-done.9.refs_4_
  112.4 2.6 %collective-permute-start.10 = (f32[25,4,128]{2,1,0:T(4,128)S(1)}, f32[25,4,128]{2,1,0:T(4,128)S(1)}, u32[]{:S(2)}, u32[]{:S(2)}) collective-permute-start(f32[25,4,128]{2,1,0:T(4,128)S(1)} %get-tuple-element.52), channel_id=1, source_target_pairs={{7,0},{0,1},{1,2},{2,3},{3,4},{4,5},{5,6},{6,7},{15,8},{8,9},{9,10... | collective-permute-start | bytes 153608 | tf_op jit(solution)/shard_map/ppermute | solution.py:480
  115.0 0.0 collective-permute-start.11
  115.0 1.8 own_more_1.3.acc_in
  116.8 0.0 collective-permute-done.10.left
  116.8 3.0 %collective-permute-done.11.right = f32[25,4,128]{2,1,0:T(4,128)S(1)} collective-permute-done((f32[25,4,128]{2,1,0:T(4,128)S(1)}, f32[25,4,128]{2,1,0:T(4,128)S(1)}, u32[]{:S(2)}, u32[]{:S(2)}) %collective-permute-start.11) | collective-permute-done | bytes 51232 | tf_op jit(solution)/shard_map/ppermute | solution.py:480
  119.7 10.2 %step_two.1 = (f32[27,6,128]{2,1,0:T(8,128)S(1)}, f32[144,128]{1,0:T(8,128)S(1)}) custom-call(f32[75,4,128]{2,1,0:T(4,128)S(1)} %get-tuple-element.51.middle, f32[25,4,128]{2,1,0:T(4,128)S(1)} %collective-permute-done.10.left, f32[25,4,128]{2,1,0:T(4,128)S(1)} %collective-permute-done.11.right, f32[27,16,128]{2,1,0:T(8,128)S(1)} %own_more_1.3.acc_in, ...), custom_call_target="tpu_custom_call" | custom-call | tf_op jit(solution)/shard_map/step_two/pallas_call | solution.py:26
  129.9 20.1 %collective-permute-start.12 = (f32[144,128]{1,0:T(8,128)S(1)}, f32[144,128]{1,0:T(8,128)S(1)}, u32[]{:S(2)}, u32[]{:S(2)}) collective-permute-start(f32[144,128]{1,0:T(8,128)S(1)} %get-tuple-element.56), channel_id=1, source_target_pairs={{8,0},{0,8},{24,16},{16,24},{40,32},{32,40},{56,48},{48,56},{9,1},... | collective-permute-start | bytes 221192 | tf_op jit(solution)/shard_map/ppermute | solution.py:469
  150.1 3.3 %collective-permute-done.12.swapped = f32[144,128]{1,0:T(8,128)S(1)} collective-permute-done((f32[144,128]{1,0:T(8,128)S(1)}, f32[144,128]{1,0:T(8,128)S(1)}, u32[]{:S(2)}, u32[]{:S(2)}) %collective-permute-start.12) | collective-permute-done | bytes 73760 | tf_op jit(solution)/shard_map/ppermute | solution.py:469
  153.4 17.7 %collective-permute-start.13 = (f32[216,128]{1,0:T(8,128)S(1)}, f32[216,128]{1,0:T(8,128)S(1)}, u32[]{:S(2)}, u32[]{:S(2)}) collective-permute-start(f32[216,128]{1,0:T(8,128)S(1)} %pack_up.1), channel_id=1, source_target_pairs={{64,0},{80,16},{96,32},{112,48},{128,64},{144,80},{160,96},{176,11... | collective-permute-start | bytes 331784 | tf_op jit(solution)/shard_map/ppermute | solution.py:465
  171.1 1.7 collective-permute-done.13.upper
  172.9 0.7 collective-permute-start.14
  173.5 0.0 collective-permute-done.14.relayed
  173.5 0.1 pack_hand_side.1
  173.6 1.5 collective-permute-start.15
  175.1 0.6 copy.10
  175.7 3.7 %collective-permute-done.15.side = f32[300,128]{1,0:T(8,128)S(1)} collective-permute-done((f32[300,128]{1,0:T(8,128)S(1)}, f32[300,128]{1,0:T(8,128)S(1)}, u32[]{:S(2)}, u32[]{:S(2)}) %collective-permute-start.15) | collective-permute-done | bytes 153632 | tf_op jit(solution)/shard_map/ppermute | solution.py:480
  179.5 2.5 %place.1 = (f32[5,5,5,3,128]{4,3,2,1,0:T(4,128)}, f32[5,5,5,3,128]{4,3,2,1,0:T(4,128)}) custom-call(s32[16]{0:T(128)} %plan_z.1, s32[8,16]{1,0:T(8,128)} %bitcast.8, s32[8,8,16]{2,1,0:T(8,128)} %bitcast.7, f32[75,6,128]{2,1,0:T(8,128)S(1)} %get-tuple-element.57.middle, f32[300,128]{1,0:T(8,128)S(1)} %collective-permute-done.15.side), custom_call_target="tpu_custom_call" | custom-call | tf_op jit(solution)/shard_map/place/pallas_call | solution.py:26
  (8 shorter events, 0.2 us)
Async XLA Ops:
  0.6 0.8 copy-start.2
  2.2 20.3 %collective-permute-start = (f32[9,4,128]{2,1,0:T(4,128)S(1)}, f32[9,4,128]{2,1,0:T(4,128)S(1)}, u32[]{:S(2)}, u32[]{:S(2)}) collective-permute-start(f32[9,4,128]{2,1,0:T(4,128)S(1)} %get-tuple-element.37), channel_id=1, source_target_pairs={{968,0},{984,16},{1000,32},{1016,48},{0,64},{16,80},{32,96},{48,11... | collective-permute-start | bytes 55304 | tf_op jit(solution)/shard_map/ppermute | solution.py:465
  5.8 17.6 %collective-permute-start.1 = (f32[9,4,128]{2,1,0:T(4,128)S(1)}, f32[9,4,128]{2,1,0:T(4,128)S(1)}, u32[]{:S(2)}, u32[]{:S(2)}) collective-permute-start(f32[9,4,128]{2,1,0:T(4,128)S(1)} %get-tuple-element.38), channel_id=1, source_target_pairs={{64,0},{80,16},{96,32},{112,48},{128,64},{144,80},{160,96},{176,11... | collective-permute-start | bytes 55304 | tf_op jit(solution)/shard_map/ppermute | solution.py:465
  23.4 14.9 %copy-start = (s32[2,3,3,3,128]{4,0,3,2,1:T(2,128)S(1)}, s32[2,3,3,3,128]{4,0,3,2,1:T(2,128)}, u32[]{:S(2)}) copy-start(s32[2,3,3,3,128]{4,0,3,2,1:T(2,128)} %param.10) | copy-start | bytes 82948
  23.5 24.5 %collective-permute-start.2 = (f32[36,4,128]{2,1,0:T(4,128)S(1)}, f32[36,4,128]{2,1,0:T(4,128)S(1)}, u32[]{:S(2)}, u32[]{:S(2)}) collective-permute-start(f32[36,4,128]{2,1,0:T(4,128)S(1)} %pack_swap.2), channel_id=1, source_target_pairs={{8,0},{0,8},{24,16},{16,24},{40,32},{32,40},{56,48},{48,56},{9,1},... | collective-permute-start | bytes 221192 | tf_op jit(solution)/shard_map/ppermute | solution.py:469
  48.0 5.9 %collective-permute-start.3 = (f32[15,4,128]{2,1,0:T(4,128)S(1)}, f32[15,4,128]{2,1,0:T(4,128)S(1)}, u32[]{:S(2)}, u32[]{:S(2)}) collective-permute-start(f32[15,4,128]{2,1,0:T(4,128)S(1)} %pack_relay.2), channel_id=1, source_target_pairs={{48,0},{24,8},{0,16},{40,24},{16,32},{56,40},{32,48},{8,56},{49,1}... | collective-permute-start | bytes 92168 | tf_op jit(solution)/shard_map/ppermute | solution.py:476
  53.9 5.3 %collective-permute-start.4 = (f32[25,4,128]{2,1,0:T(4,128)S(1)}, f32[25,4,128]{2,1,0:T(4,128)S(1)}, u32[]{:S(2)}, u32[]{:S(2)}) collective-permute-start(f32[25,4,128]{2,1,0:T(4,128)S(1)} %get-tuple-element.40), channel_id=1, source_target_pairs={{7,0},{0,1},{1,2},{2,3},{3,4},{4,5},{5,6},{6,7},{15,8},{8,9},{9,10... | collective-permute-start | bytes 153608 | tf_op jit(solution)/shard_map/ppermute | solution.py:480
  57.5 4.8 %copy-start.1 = (f32[3,3,3,3,128]{4,3,2,1,0:T(4,128)S(1)}, f32[3,3,3,3,128]{4,3,2,1,0:T(4,128)}, u32[]{:S(2)}) copy-start(f32[3,3,3,3,128]{4,3,2,1,0:T(4,128)} %vel.1) | copy-start | bytes 124420
  57.5 4.7 %collective-permute-start.5 = (f32[25,4,128]{2,1,0:T(4,128)S(1)}, f32[25,4,128]{2,1,0:T(4,128)S(1)}, u32[]{:S(2)}, u32[]{:S(2)}) collective-permute-start(f32[25,4,128]{2,1,0:T(4,128)S(1)} %get-tuple-element.41), channel_id=1, source_target_pairs={{1,0},{2,1},{3,2},{4,3},{5,4},{6,5},{7,6},{0,7},{9,8},{10,9},{11,1... | collective-permute-start | bytes 153608 | tf_op jit(solution)/shard_map/ppermute | solution.py:480
  72.5 7.5 %collective-permute-start.6 = (f32[9,4,128]{2,1,0:T(4,128)S(1)}, f32[9,4,128]{2,1,0:T(4,128)S(1)}, u32[]{:S(2)}, u32[]{:S(2)}) collective-permute-start(f32[9,4,128]{2,1,0:T(4,128)S(1)} %get-tuple-element.49), channel_id=1, source_target_pairs={{968,0},{984,16},{1000,32},{1016,48},{0,64},{16,80},{32,96},{48,11... | collective-permute-start | bytes 55304 | tf_op jit(solution)/shard_map/ppermute | solution.py:465
  74.4 6.4 %collective-permute-start.7 = (f32[9,4,128]{2,1,0:T(4,128)S(1)}, f32[9,4,128]{2,1,0:T(4,128)S(1)}, u32[]{:S(2)}, u32[]{:S(2)}) collective-permute-start(f32[9,4,128]{2,1,0:T(4,128)S(1)} %get-tuple-element.50), channel_id=1, source_target_pairs={{64,0},{80,16},{96,32},{112,48},{128,64},{144,80},{160,96},{176,11... | collective-permute-start | bytes 55304 | tf_op jit(solution)/shard_map/ppermute | solution.py:465
  80.9 25.6 %collective-permute-start.8 = (f32[36,4,128]{2,1,0:T(4,128)S(1)}, f32[36,4,128]{2,1,0:T(4,128)S(1)}, u32[]{:S(2)}, u32[]{:S(2)}) collective-permute-start(f32[36,4,128]{2,1,0:T(4,128)S(1)} %pack_swap.3), channel_id=1, source_target_pairs={{8,0},{0,8},{24,16},{16,24},{40,32},{32,40},{56,48},{48,56},{9,1},... | collective-permute-start | bytes 221192 | tf_op jit(solution)/shard_map/ppermute | solution.py:469
  106.5 5.8 %collective-permute-start.9 = (f32[15,4,128]{2,1,0:T(4,128)S(1)}, f32[15,4,128]{2,1,0:T(4,128)S(1)}, u32[]{:S(2)}, u32[]{:S(2)}) collective-permute-start(f32[15,4,128]{2,1,0:T(4,128)S(1)} %pack_relay.3), channel_id=1, source_target_pairs={{48,0},{24,8},{0,16},{40,24},{16,32},{56,40},{32,48},{8,56},{49,1}... | collective-permute-start | bytes 92168 | tf_op jit(solution)/shard_map/ppermute | solution.py:476
  112.4 4.4 %collective-permute-start.10 = (f32[25,4,128]{2,1,0:T(4,128)S(1)}, f32[25,4,128]{2,1,0:T(4,128)S(1)}, u32[]{:S(2)}, u32[]{:S(2)}) collective-permute-start(f32[25,4,128]{2,1,0:T(4,128)S(1)} %get-tuple-element.52), channel_id=1, source_target_pairs={{7,0},{0,1},{1,2},{2,3},{3,4},{4,5},{5,6},{6,7},{15,8},{8,9},{9,10... | collective-permute-start | bytes 153608 | tf_op jit(solution)/shard_map/ppermute | solution.py:480
  115.0 4.7 %collective-permute-start.11 = (f32[25,4,128]{2,1,0:T(4,128)S(1)}, f32[25,4,128]{2,1,0:T(4,128)S(1)}, u32[]{:S(2)}, u32[]{:S(2)}) collective-permute-start(f32[25,4,128]{2,1,0:T(4,128)S(1)} %get-tuple-element.53), channel_id=1, source_target_pairs={{1,0},{2,1},{3,2},{4,3},{5,4},{6,5},{7,6},{0,7},{9,8},{10,9},{11,1... | collective-permute-start | bytes 153608 | tf_op jit(solution)/shard_map/ppermute | solution.py:480
  129.9 23.4 %collective-permute-start.12 = (f32[144,128]{1,0:T(8,128)S(1)}, f32[144,128]{1,0:T(8,128)S(1)}, u32[]{:S(2)}, u32[]{:S(2)}) collective-permute-start(f32[144,128]{1,0:T(8,128)S(1)} %get-tuple-element.56), channel_id=1, source_target_pairs={{8,0},{0,8},{24,16},{16,24},{40,32},{32,40},{56,48},{48,56},{9,1},... | collective-permute-start | bytes 221192 | tf_op jit(solution)/shard_map/ppermute | solution.py:469
  153.4 19.4 %collective-permute-start.13 = (f32[216,128]{1,0:T(8,128)S(1)}, f32[216,128]{1,0:T(8,128)S(1)}, u32[]{:S(2)}, u32[]{:S(2)}) collective-permute-start(f32[216,128]{1,0:T(8,128)S(1)} %pack_up.1), channel_id=1, source_target_pairs={{64,0},{80,16},{96,32},{112,48},{128,64},{144,80},{160,96},{176,11... | collective-permute-start | bytes 331784 | tf_op jit(solution)/shard_map/ppermute | solution.py:465
  172.9 0.7 collective-permute-start.14
  173.6 5.9 %collective-permute-start.15 = (f32[300,128]{1,0:T(8,128)S(1)}, f32[300,128]{1,0:T(8,128)S(1)}, u32[]{:S(2)}, u32[]{:S(2)}) collective-permute-start(f32[300,128]{1,0:T(8,128)S(1)} %get-tuple-element.58), channel_id=1, source_target_pairs={{1,0},{2,1},{3,2},{4,3},{5,4},{6,5},{7,6},{0,7},{9,8},{10,9},{11,1... | collective-permute-start | bytes 460808 | tf_op jit(solution)/shard_map/ppermute | solution.py:480
